TPU v7x, 32 devices: a whole 2x2x4 slice. The times are simulated.
32 devices in a mesh: shard: 2 (over x), ctx: 4 (over y, core), tp: 4 (over z).
Axes of the slice: x: 2, y: 2, z: 4, core: 2. Of those that a mesh axis runs over, the one named last changes fastest.
Arguments:
- tokens: bfloat16 [8, 1024, 767], P('shard', 'ctx'), may hold values from -6 to 6
- lengths: int32 [8], P('shard'), may hold values from 256 to 1024, as said below
- first_gain: float32 [768], replicated, may hold values from 0.5 to 1.5
- entry_weight: bfloat16 [3, 768, 768], P(None, ('shard', 'ctx'), 'tp'), may hold values from -0.21875 to 0.21875
- entry_bias: float32 [2, 768], P(None, 'tp'), may hold values from -3 to 3
- exit_weight: bfloat16 [768, 768], P('tp', ('shard', 'ctx')), may hold values from -0.625 to 0.625
- exit_bias: float32 [768], replicated, may hold values from -3 to 3
- second_gain: float32 [768], replicated, may hold values from 0.5 to 1.5
- hidden_weight: bfloat16 [768, 3072], P(('shard', 'ctx'), 'tp'), may hold values from -0.21875 to 0.21875
- hidden_bias: float32 [3072], P('tp'), may hold values from -3 to 3
- return_weight: bfloat16 [3072, 768], P('tp', ('shard', 'ctx')), may hold values from -0.109375 to 0.109375
- return_bias: float32 [768], replicated, may hold values from -3 to 3
- cotangent: bfloat16 [8, 1024, 767], P('shard', 'ctx'), may hold values from -6 to 6
Outputs:
- result: bfloat16 [8, 1024, 767], P('shard', 'ctx')
- tokens_gradient: bfloat16 [8, 1024, 767], P('shard', 'ctx')
- first_gain_gradient: float32 [768], replicated
- entry_weight_gradient: float32 [3, 768, 768], P(None, ('shard', 'ctx'), 'tp')
- entry_bias_gradient: float32 [2, 768], P(None, 'tp')
- exit_weight_gradient: float32 [768, 768], P('tp', ('shard', 'ctx'))
- exit_bias_gradient: float32 [768], replicated
- second_gain_gradient: float32 [768], replicated
- hidden_weight_gradient: float32 [768, 3072], P(('shard', 'ctx'), 'tp')
- hidden_bias_gradient: float32 [3072], P('tp')
- return_weight_gradient: float32 [3072, 768], P('tp', ('shard', 'ctx'))
- return_bias_gradient: float32 [768], replicated
Inputs may be any that keep to these rules, and one draw needn't show every extreme that they name: `lengths`: in every draw some sequence has exactly 1024 valid positions and some has exactly 256.
All inputs are finite; a program needn't handle non-finite values.
Results may differ from a plain program's by a relative error of at most 0.014.
Values may be sent and summed in bfloat16 or wider, within the bound.
No kernel may reach another device: no remote copies, remote signals or barrier semaphores. Data moves between devices by JAX's collectives and lax.ppermute only.
A program may use at most 256 MiB of HBM per device.

v0:
```python
import math

import jax
import jax.numpy as jnp
from jax import lax
from jax.sharding import PartitionSpec as P

HDIM = 64


EPSILON = 1e-05


def row_mean(values):
    return jnp.mean(values, -1, keepdims=True)


def shards(
    tokens,
    lengths,
    first_gain,
    entry_weight,
    entry_bias,
    exit_weight,
    exit_bias,
    second_gain,
    hidden_weight,
    hidden_bias,
    return_weight,
    return_bias,
    cotangent,
):
    seq_dev, local, narrow = tokens.shape
    row_count = seq_dev * local
    full_len = local * lax.axis_size("ctx")
    head_width = entry_weight.shape[2]
    heads_here = head_width // HDIM
    scale = 1.0 / math.sqrt(HDIM)
    bfloat = jnp.bfloat16
    single = jnp.float32
    full_entry, full_exit, full_hidden, full_return = (
        lax.all_gather(entry_weight, ("shard", "ctx"), axis=1, tiled=True),
        lax.all_gather(exit_weight, ("shard", "ctx"), axis=1, tiled=True),
        lax.all_gather(hidden_weight, ("shard", "ctx"), axis=0, tiled=True),
        lax.all_gather(return_weight, ("shard", "ctx"), axis=1, tiled=True),
    )
    stream_part = tokens.astype(single).reshape(row_count, narrow)
    stream = jnp.concatenate([stream_part, -jnp.sum(stream_part, -1, keepdims=True)], 1)
    first_inverse = lax.rsqrt(row_mean(stream * stream) + EPSILON)
    first_unit = stream * first_inverse
    first_normed = (first_unit * first_gain).astype(bfloat)
    queries = (
        jnp.dot(first_normed, full_entry[0], preferred_element_type=single) + entry_bias[0]
    ).astype(bfloat)
    keys = jnp.dot(first_normed, full_entry[1], preferred_element_type=single).astype(bfloat)
    values = (
        jnp.dot(first_normed, full_entry[2], preferred_element_type=single) + entry_bias[1]
    ).astype(bfloat)
    seq_shape = (seq_dev, local, head_width)
    all_keys, all_values = (
        lax.all_gather(keys.reshape(seq_shape), "ctx", axis=1, tiled=True),
        lax.all_gather(values.reshape(seq_shape), "ctx", axis=1, tiled=True),
    )
    offset = lax.axis_index("ctx") * local
    query_pos = offset + jnp.arange(local, dtype=jnp.int32)
    key_pos = jnp.arange(full_len, dtype=jnp.int32)
    local_heads = (seq_dev, local, heads_here, HDIM)
    full_heads = (seq_dev, full_len, heads_here, HDIM)
    allowed = (
        (key_pos[None, None, :] <= query_pos[None, :, None])
        & (key_pos[None, None, :] < lengths[:, None, None])
    )[:, None]

    def masked_scores(query_block, key_block):
        raw_scores = (
            jnp.einsum("sqhd,skhd->shqk", query_block, key_block, preferred_element_type=single)
            * scale
        )
        return jnp.where(allowed, raw_scores, -1e30)

    query_heads = queries.reshape(local_heads)
    scores = masked_scores(query_heads, all_keys.reshape(full_heads))
    largest = jnp.max(scores, -1, keepdims=True)
    exponent = jnp.exp(scores - largest)
    totals = jnp.sum(exponent, -1, keepdims=True)
    weights = (exponent / totals).astype(bfloat)
    log_totals = largest + jnp.log(totals)
    attended = jnp.einsum(
        "shqk,skhd->sqhd", weights, all_values.reshape(full_heads), preferred_element_type=single
    ).astype(bfloat)
    attended_rows = attended.reshape(row_count, head_width)
    exit_term = jnp.dot(attended_rows, full_exit, preferred_element_type=single)
    branch = lax.psum(exit_term, "tp") + exit_bias
    middle = stream + branch - row_mean(branch)
    second_inverse = lax.rsqrt(row_mean(middle * middle) + EPSILON)
    second_unit = middle * second_inverse
    second_normed = (second_unit * second_gain).astype(bfloat)
    hidden = jnp.dot(second_normed, full_hidden, preferred_element_type=single) + hidden_bias
    activated, gelu_pull = jax.vjp(
        lambda values_in: jax.nn.gelu(values_in, approximate=True), hidden
    )
    activated_low = activated.astype(bfloat)
    return_term = jnp.dot(activated_low, full_return, preferred_element_type=single)
    returned = lax.psum(return_term.astype(jnp.bfloat16), "tp").astype(jnp.float32) + return_bias
    full_stream = middle + returned - row_mean(returned)
    result_rows = full_stream[:, :narrow].astype(bfloat)
    result = result_rows.reshape(seq_dev, local, narrow)
    full_entry, full_exit, full_hidden, full_return = (
        lax.all_gather(entry_weight, ("shard", "ctx"), axis=1, tiled=True),
        lax.all_gather(exit_weight, ("shard", "ctx"), axis=1, tiled=True),
        lax.all_gather(hidden_weight, ("shard", "ctx"), axis=0, tiled=True),
        lax.all_gather(return_weight, ("shard", "ctx"), axis=1, tiled=True),
    )
    valid = (query_pos[None, :] < lengths[:, None]).astype(single).reshape(row_count, 1)
    cot_rows = cotangent.astype(single).reshape(row_count, narrow) * valid
    cot_full = jnp.concatenate([cot_rows, jnp.zeros((row_count, 1), single)], 1)
    returned_grad = (cot_full - row_mean(cot_full)).astype(bfloat)
    return_bias_grad = jnp.sum(returned_grad.astype(single), 0)
    return_weight_grad = jnp.einsum(
        "rf,rd->fd", activated_low, returned_grad, preferred_element_type=single
    )
    activated_grad = jnp.einsum(
        "rd,fd->rf", returned_grad, full_return, preferred_element_type=single
    )
    hidden_grad = gelu_pull(activated_grad)[0].astype(bfloat)
    hidden_bias_grad = jnp.sum(hidden_grad.astype(single), 0)
    hidden_weight_grad = jnp.einsum(
        "rd,rf->df", second_normed, hidden_grad, preferred_element_type=single
    )
    second_term = jnp.einsum("rf,df->rd", hidden_grad, full_hidden, preferred_element_type=single)
    second_grad = lax.psum(second_term, "tp")
    second_gain_grad = jnp.sum(second_grad * second_unit, 0)
    second_scaled = second_grad * second_gain
    middle_grad = cot_full + second_inverse * (
        second_scaled - second_unit * row_mean(second_scaled * second_unit)
    )
    branch_grad = (middle_grad - row_mean(middle_grad)).astype(bfloat)
    exit_bias_grad = jnp.sum(branch_grad.astype(single), 0)
    exit_weight_grad = jnp.einsum(
        "re,rd->ed", attended_rows, branch_grad, preferred_element_type=single
    )
    attended_grad = jnp.einsum(
        "rd,ed->re", branch_grad, full_exit, preferred_element_type=single
    ).astype(bfloat)
    all_keys, all_values = (
        lax.all_gather(keys.reshape(seq_shape), "ctx", axis=1, tiled=True),
        lax.all_gather(values.reshape(seq_shape), "ctx", axis=1, tiled=True),
    )
    key_heads = all_keys.reshape(full_heads)
    value_heads = all_values.reshape(full_heads)
    out_grad = attended_grad.reshape(local_heads)
    back_scores = masked_scores(query_heads, key_heads)
    probs = jnp.exp(back_scores - log_totals)
    probs_low = probs.astype(bfloat)
    prob_rounded = lax.optimization_barrier(
        jnp.einsum("sqhd,skhd->shqk", out_grad, value_heads, preferred_element_type=single).astype(
            bfloat
        )
    )
    prob_grad = prob_rounded.astype(single)
    inner = jnp.sum(probs * prob_grad, -1, keepdims=True)
    score_grad = (probs * (prob_grad - inner)).astype(bfloat)
    query_grads = (
        jnp.einsum("shqk,skhd->sqhd", score_grad, key_heads, preferred_element_type=single) * scale
    ).astype(bfloat)
    key_parts = (
        jnp.einsum("shqk,sqhd->skhd", score_grad, query_heads, preferred_element_type=single)
        * scale
    )
    value_parts = jnp.einsum("shqk,sqhd->skhd", probs_low, out_grad, preferred_element_type=single)
    key_sums, value_sums = (
        lax.psum_scatter(
            key_parts.reshape(seq_dev, full_len, head_width), "ctx", scatter_dimension=1, tiled=True
        ),
        lax.psum_scatter(
            value_parts.reshape(seq_dev, full_len, head_width),
            "ctx",
            scatter_dimension=1,
            tiled=True,
        ),
    )
    query_low = query_grads.reshape(row_count, head_width)
    key_low = key_sums.reshape(row_count, head_width).astype(bfloat)
    value_low = value_sums.reshape(row_count, head_width).astype(bfloat)
    entry_bias_grad = jnp.stack(
        [jnp.sum(query_low.astype(single), 0), jnp.sum(value_low.astype(single), 0)]
    )
    entry_weight_grad = jnp.stack(
        [
            jnp.einsum("rd,re->de", first_normed, query_low, preferred_element_type=single),
            jnp.einsum("rd,re->de", first_normed, key_low, preferred_element_type=single),
            jnp.einsum("rd,re->de", first_normed, value_low, preferred_element_type=single),
        ]
    )
    first_part = (
        jnp.einsum("re,de->rd", query_low, full_entry[0], preferred_element_type=single)
        + jnp.einsum("re,de->rd", key_low, full_entry[1], preferred_element_type=single)
        + jnp.einsum("re,de->rd", value_low, full_entry[2], preferred_element_type=single)
    )
    first_grad = lax.psum(first_part, "tp")
    first_gain_grad = jnp.sum(first_grad * first_unit, 0)
    first_scaled = first_grad * first_gain
    stream_grad = middle_grad + first_inverse * (
        first_scaled - first_unit * row_mean(first_scaled * first_unit)
    )
    tokens_rows = (stream_grad[:, :narrow] - stream_grad[:, narrow:]).astype(bfloat)
    tokens_grad = tokens_rows.reshape(seq_dev, local, narrow)
    weight_grads = (
        lax.psum_scatter(entry_weight_grad, ("shard", "ctx"), scatter_dimension=1, tiled=True),
        lax.psum_scatter(exit_weight_grad, ("shard", "ctx"), scatter_dimension=1, tiled=True),
        lax.psum_scatter(hidden_weight_grad, ("shard", "ctx"), scatter_dimension=0, tiled=True),
        lax.psum_scatter(return_weight_grad, ("shard", "ctx"), scatter_dimension=1, tiled=True),
    )
    small_grads = lax.psum(
        (
            first_gain_grad,
            entry_bias_grad,
            exit_bias_grad,
            second_gain_grad,
            hidden_bias_grad,
            return_bias_grad,
        ),
        ("shard", "ctx"),
    )
    return (
        result,
        tokens_grad,
        small_grads[0],
        weight_grads[0],
        small_grads[1],
        weight_grads[1],
        small_grads[2],
        small_grads[3],
        weight_grads[2],
        small_grads[4],
        weight_grads[3],
        small_grads[5],
    )


def solution(mesh):
    return jax.shard_map(
        shards,
        mesh=mesh,
        in_specs=(
            P("shard", "ctx", None),
            P("shard"),
            P(),
            P(None, ("shard", "ctx"), "tp"),
            P(None, "tp"),
            P("tp", ("shard", "ctx")),
            P(),
            P(),
            P(("shard", "ctx"), "tp"),
            P("tp"),
            P("tp", ("shard", "ctx")),
            P(),
            P("shard", "ctx", None),
        ),
        out_specs=(
            P("shard", "ctx", None),
            P("shard", "ctx", None),
            P(),
            P(None, ("shard", "ctx"), "tp"),
            P(None, "tp"),
            P("tp", ("shard", "ctx")),
            P(),
            P(),
            P(("shard", "ctx"), "tp"),
            P("tp"),
            P("tp", ("shard", "ctx")),
            P(),
        ),
        check_vma=False,
    )
```

profile of v0, /device:TPU:0, one launch (start us, length us, event | category | flops | bytes accessed | tf_op | source)
XLA Modules:
  0.0 1059.6 jit_solution(7665863335763462059)
XLA Ops:
  8.1 2.3 convert_reduce_fusion.5
  10.3 2.9 copy.52
  14.5 13.1 %all_gather.24 = bf16[3,768,192]{2,1,0:T(8,128)(2,1)S(1)} all-gather(bf16[3,96,192]{2,1,0:T(8,128)(2,1)S(1)} %copy-done.38), channel_id=1, replica_groups=mesh['shard'=2,'ctx'=4,'tp'=4] {'shard','ctx'}, dimensions={1}, use_global_device_ids=true | all-gather | bytes 995328 | tf_op jit(solution)/shard_map/all_gather | solution.py:42
  36.3 2.9 fusion.21
  42.1 12.4 %all_gather.27 = bf16[192,768]{0,1:T(8,128)(2,1)} all-gather(bf16[192,96]{0,1:T(8,128)(2,1)} %copy.58), channel_id=1, replica_groups=mesh['shard'=2,'ctx'=4,'tp'=4] {'shard','ctx'}, dimensions={1}, use_global_device_ids=true | all-gather | bytes 331776 | tf_op jit(solution)/shard_map/all_gather | solution.py:43
  58.7 2.9 fusion.38
  61.6 4.6 copy-done
  66.2 3.4 fusion.3
  69.5 6.5 all-gather.5.cloned.1.call-done
  78.0 6.6 fusion.24
  85.7 2.2 fusion.39
  89.5 4.3 copy.59
  93.8 2.2 bitcast_multiply_fusion
  99.8 109.4 %all-reduce.7.cloned.1.call-done = f32[1024,768]{1,0:T(8,128)} async-done(((f32[1024,768]{1,0:T(8,128)}), f32[1024,768]{1,0:T(8,128)}) %all-reduce.7.cloned.1.call-update) | async-done | bytes 3145744 | tf_op jit(solution)/shard_map/psum | solution.py:93
  209.2 2.2 add_reduce_fusion
  211.5 4.3 multiply_reduce_fusion.4
  215.8 5.5 fusion.33
  221.3 5.6 convert_reduce_fusion.1
  228.1 3.1 fusion.40
  232.3 119.0 %all-reduce.11.cloned.1.call-done = f32[1024,768]{1,0:T(8,128)} async-done(((f32[1024,768]{1,0:T(8,128)}), f32[1024,768]{1,0:T(8,128)}) %all-reduce.11.cloned.1.call-update) | async-done | bytes 3145744 | tf_op jit(solution)/shard_map/psum | solution.py:131
  351.4 3.5 multiply_reduce_fusion
  363.3 7.6 fusion
  371.0 3.0 fusion.2
  376.6 48.2 %copy.69 = f32[4,1024,192]{0,2,1:T(8,128)} copy(f32[4,1024,192]{1,2,0:T(8,128)S(1)} %bitcast.133) | data formatting | bytes 6291456
  424.8 84.3 %reshape.241 = f32[1024,768]{1,0:T(8,128)} reshape(f32[1024,192,4]{2,1,0:T(8,128)} %bitcast.22) | data formatting | bytes 6291456
  509.5 6.1 fusion.5
  515.6 48.3 %copy.71 = f32[4,1024,192]{0,2,1:T(8,128)} copy(f32[4,1024,192]{1,2,0:T(8,128)S(1)} %bitcast.127) | data formatting | bytes 6291456
  563.9 84.3 %reshape.243 = f32[1024,768]{1,0:T(8,128)} reshape(f32[1024,192,4]{2,1,0:T(8,128)} %bitcast.25) | data formatting | bytes 6291456
  649.5 5.1 convolution_convert_fusion.1
  656.9 5.0 convert_reduce_fusion.4
  663.5 29.2 %reshape.242 = bf16[256,192,4]{2,1,0:T(8,128)(2,1)} reshape(f32[256,768]{1,0:T(8,128)} %reduce-scatter.19.cloned.1.call-done) | data formatting | bytes 1179648
  692.7 12.2 %copy.70 = bf16[4,256,192]{1,0,2:T(4,128)(2,1)S(1)} copy(bf16[4,256,192]{0,2,1:T(8,128)(2,1)} %bitcast.123) | data formatting | bytes 786432
  705.0 29.3 %reshape.244 = bf16[256,192,4]{2,1,0:T(8,128)(2,1)} reshape(f32[256,768]{1,0:T(8,128)} %reduce-scatter.21.cloned.1.call-done) | data formatting | bytes 1179648
  734.3 12.2 %copy.72 = bf16[4,256,192]{1,0,2:T(4,128)(2,1)S(1)} copy(bf16[4,256,192]{0,2,1:T(8,128)(2,1)} %bitcast.124) | data formatting | bytes 786432
  748.9 2.9 copy.73
  751.9 2.9 reshape.245
  757.5 2.3 add_add_fusion
  760.0 5.8 fusion.34
  765.9 4.4 fusion.32
  773.7 3.9 copy.66
  777.7 15.9 %reduce-scatter.25.cloned.1.call-done = f32[96,192]{1,0:T(8,128)} async-done(((f32[768,192]{1,0:T(8,128)}), f32[96,192]{1,0:T(8,128)}) %reduce-scatter.25.cloned.1.call-update) | async-done | bytes 73744
  796.2 40.9 %reduce-scatter.23.cloned.1.call-done = f32[96,576]{1,0:T(8,128)} async-done(((f32[768,576]{1,0:T(8,128)}), f32[96,576]{1,0:T(8,128)}) %reduce-scatter.23.cloned.1.call-update) | async-done | bytes 221200
  839.1 121.4 %all-reduce.13.cloned.1.call-done = f32[1024,768]{1,0:T(8,128)} async-done(((f32[1024,768]{1,0:T(8,128)}), f32[1024,768]{1,0:T(8,128)}) %all-reduce.13.cloned.1.call-update) | async-done | bytes 3145744 | tf_op jit(solution)/shard_map/psum | solution.py:200
  960.5 3.0 multiply_reduce_fusion.1
  966.7 2.2 copy.67
  968.9 25.0 %all-reduce.1 = (f32[768]{0:T(1024)}, f32[2,192]{1,0:T(2,128)}, f32[768]{0:T(1024)}, f32[768]{0:T(1024)}, f32[768]{0:T(1024)}, /*index=5*/f32[768]{0:T(1024)}) all-reduce(f32[768]{0:T(1024)S(1)} %get-tuple-element.48, f32[2,192]{1,0:T(2,128)S(1)} %pad_maximum_fusion.2, ...), channel_id=1, replica_groups=mesh['shard'=2,'ctx'=4,'tp'=4] {'shard','ctx'}, use_global_device_ids=true, to_apply=%region_19.20 | all-reduce | flops 4224 | bytes 33792 | tf_op jit(solution)/shard_map/psum | solution.py:214
  993.9 11.9 %reduce-scatter.17.cloned.1.call-done = f32[768,96]{0,1:T(8,128)} async-done(((f32[768,768]{0,1:T(8,128)}), f32[768,96]{0,1:T(8,128)}) %reduce-scatter.17.cloned.1.call-update) | async-done | bytes 294928 | tf_op jit(solution)/shard_map/reduce_scatter | solution.py:212
  1005.8 46.2 %reduce-scatter.15.cloned.1.call-done = f32[96,768]{1,0:T(8,128)} async-done(((f32[768,768]{1,0:T(8,128)}), f32[96,768]{1,0:T(8,128)}) %reduce-scatter.15.cloned.1.call-update) | async-done | bytes 294928 | tf_op jit(solution)/shard_map/reduce_scatter | solution.py:211
  (233 shorter events, 60.2 us)
Async XLA Ops:
  8.0 6.5 copy-start.38
  8.0 48.6 %all-gather.7.cloned.1.call-start = ((), (), s32[]{:S(2)}) async-start(), calls=%async_computation.7 | async-start | bytes 1966080 | tf_op jit(solution)/shard_map/all_gather | solution.py:61
  13.3 198.2 %copy-start.1 = (f32[4,256,767]{2,1,0:T(8,128)}, f32[4,256,767]{2,1,0:T(8,128)S(1)}, u32[]{:S(2)}) copy-start(f32[4,256,767]{2,1,0:T(8,128)S(1)} %copy.52) | copy-start | bytes 9424900
  13.3 16.2 %copy-start.45 = (f32[768]{0:T(1024)S(1)}, f32[768]{0:T(1024)}, u32[]{:S(2)}) copy-start(f32[768]{0:T(1024)} %param.15) | copy-start | bytes 9220
  14.5 15.0 %copy-start.14 = (f32[1,1024]{0,1:T(8,128)S(1)}, f32[1,1024]{0,1:T(8,128)}, u32[]{:S(2)}) copy-start(f32[1,1024]{0,1:T(8,128)} %copy.81) | copy-start | bytes 12292
  33.0 43.1 %all-gather.5.cloned.1.call-start = ((), (), s32[]{:S(2)}) async-start(), calls=%async_computation.6 | async-start | bytes 1966080 | tf_op jit(solution)/shard_map/all_gather | solution.py:62
  33.1 21.4 %copy-start.59 = (s32[4]{0:T(128)S(1)}, s32[4]{0:T(128)}, u32[]{:S(2)}) copy-start(s32[4]{0:T(128)} %param.14) | copy-start | bytes 52
  36.3 172.9 %all-reduce.7.cloned.1.call-start = ((), (), s32[]{:S(2)}) async-start(), calls=%async_computation.8 | async-start | bytes 6291456 | tf_op jit(solution)/shard_map/psum | solution.py:93
  42.1 19.5 %copy-start.26 = (bf16[4,256,3,64]{1,0,3,2:T(4,128)(2,1)}, bf16[4,256,3,64]{1,0,3,2:T(4,128)(2,1)S(1)}, u32[]{:S(2)}) copy-start(bf16[4,256,3,64]{1,0,3,2:T(4,128)(2,1)S(1)} %reshape.226) | copy-start | bytes 1179652
  61.5 4.6 copy-start
  61.6 16.4 %copy-start.37 = (f32[4,3,256]{2,1,0:T(4,128)}, f32[4,3,256]{2,1,0:T(4,128)S(1)}, u32[]{:S(2)}) copy-start(f32[4,3,256]{2,1,0:T(4,128)S(1)} %get-tuple-element.72) | copy-start | bytes 36868
  78.0 6.6 copy-start.23
  78.0 7.7 copy-start.30
  88.0 127.8 %all-gather.9.cloned.1.call-start = ((), (), s32[]{:S(2)}) async-start(), calls=%async_computation.9 | async-start | bytes 1327104 | tf_op jit(solution)/shard_map/all_gather | solution.py:44
  88.6 132.7 %all-gather.11.cloned.1.call-start = ((), (), s32[]{:S(2)}) async-start(), calls=%async_computation.10 | async-start | bytes 1327104 | tf_op jit(solution)/shard_map/all_gather | solution.py:45
  89.2 262.2 %all-reduce.11.cloned.1.call-start = ((), (), s32[]{:S(2)}) async-start(), calls=%async_computation.12 | async-start | bytes 6291456 | tf_op jit(solution)/shard_map/psum | solution.py:131
  96.3 113.0 %copy-start.47 = (f32[768]{0:T(1024)S(1)}, f32[768]{0:T(1024)}, u32[]{:S(2)}) copy-start(f32[768]{0:T(1024)} %param.19) | copy-start | bytes 9220
  211.5 4.3 copy-start.48
  215.7 5.5 copy-start.42
  215.8 5.5 copy-start.36
  215.8 5.5 copy-start.63
  221.3 6.8 copy-start.62
  231.1 120.2 %copy-start.6 = (f32[1024,768]{1,0:T(8,128)S(1)}, f32[1024,768]{1,0:T(8,128)}, u32[]{:S(2)}) copy-start(f32[1024,768]{1,0:T(8,128)} %get-tuple-element.67) | copy-start | bytes 9437188
  231.2 432.3 %reduce-scatter.19.cloned.1.call-start = ((), (), s32[]{:S(2)}) async-start(), calls=%async_computation.16 | async-start | bytes 3932160
  351.4 3.8 copy-start.43
  361.5 9.5 slice-start
  361.5 9.5 slice-start.1
  363.3 7.6 slice-start.2
  509.2 195.9 %reduce-scatter.21.cloned.1.call-start = ((), (), s32[]{:S(2)}) async-start(), calls=%async_computation.17 | async-start | bytes 3932160
  648.2 6.4 copy-start.18
  648.2 6.4 copy-start.35
  648.3 122.1 %all-reduce.9.cloned.1.call-start = ((), (), s32[]{:S(2)}) async-start(), calls=%async_computation.11 | async-start | bytes 3145728 | tf_op jit(solution)/shard_map/psum | solution.py:104
  654.6 138.9 %reduce-scatter.25.cloned.1.call-start = ((), (), s32[]{:S(2)}) async-start(), calls=%async_computation.19 | async-start | bytes 884736
  656.3 6.7 copy-start.5
  656.3 180.8 %reduce-scatter.23.cloned.1.call-start = ((), (), s32[]{:S(2)}) async-start(), calls=%async_computation.18 | async-start | bytes 2211840
  705.0 41.6 %copy-start.32 = (bf16[24,8,4,256]{3,1,2,0:T(8,128)(2,1)}, bf16[24,8,4,256]{3,1,2,0:T(8,128)(2,1)S(1)}, u32[]{:S(2)}) copy-start(bf16[24,8,4,256]{3,1,2,0:T(8,128)(2,1)S(1)} %copy.85) | copy-start | bytes 1179652
  754.8 205.7 %all-reduce.13.cloned.1.call-start = ((), (), s32[]{:S(2)}) async-start(), calls=%async_computation.13 | async-start | bytes 6291456 | tf_op jit(solution)/shard_map/psum | solution.py:200
  759.9 6.0 copy-start.7
  759.9 6.0 copy-start.44
  759.9 6.0 copy-start.50
  759.9 245.9 %reduce-scatter.17.cloned.1.call-start = ((), (), s32[]{:S(2)}) async-start(), calls=%async_computation.15 | async-start | bytes 2654208 | tf_op jit(solution)/shard_map/reduce_scatter | solution.py:212
  765.8 4.6 copy-start.54
  765.8 286.2 %reduce-scatter.15.cloned.1.call-start = ((), (), s32[]{:S(2)}) async-start(), calls=%async_computation.14 | async-start | bytes 2654208 | tf_op jit(solution)/shard_map/reduce_scatter | solution.py:211
  772.2 23.0 %copy-start.29 = (bf16[4,256,192]{1,0,2:T(4,128)(2,1)S(1)}, bf16[4,256,192]{1,0,2:T(4,128)(2,1)}, u32[]{:S(2)}) copy-start(bf16[4,256,192]{1,0,2:T(4,128)(2,1)} %copy-done.28) | copy-start | bytes 1179652
  773.7 186.8 %copy-start.2 = (f32[4,256,767]{2,1,0:T(8,128)S(1)}, f32[4,256,767]{2,1,0:T(8,128)}, u32[]{:S(2)}) copy-start(f32[4,256,767]{2,1,0:T(8,128)} %copy-done.1) | copy-start | bytes 9424900
  773.7 186.8 %copy-start.41 = (f32[1024]{0:T(1024)S(1)}, f32[1024]{0:T(1024)}, u32[]{:S(2)}) copy-start(f32[1024]{0:T(1024)} %copy-done.40) | copy-start | bytes 12292
  773.7 186.8 %copy-start.46 = (f32[768]{0:T(1024)S(1)}, f32[768]{0:T(1024)}, u32[]{:S(2)}) copy-start(f32[768]{0:T(1024)} %param.15) | copy-start | bytes 9220
  960.5 4.1 copy-start.20
  (35 other events, 77.8 us)
Sparse Core Ops, SparseCore 0:
  33.1 21.5 all-gather.6
  56.2 19.8 all-gather.4
  88.1 121.0 all-reduce.6
  231.3 120.0 all-reduce.10
  509.3 36.8 reduce-scatter.18
  648.4 36.5 reduce-scatter.20
  687.3 68.9 all-reduce.8
  759.5 34.0 reduce-scatter.24
  797.0 40.1 reduce-scatter.22
  839.4 121.0 all-reduce.12
  964.4 41.4 reduce-scatter.16
  1009.6 42.3 reduce-scatter.14
Sparse Core Ops, SparseCore 1:
  90.4 23.8 all-gather.8
  116.0 23.8 all-gather.10
where the time goes:
time: 1070 us; the launch traced here: 1060 us
  waiting for transfers between devices  473 us (44%)
  local copies, waits for them, and re-layouts  400 us (37%)
  matrix products  69.6 us (7%)
  blocking collectives  50.5 us (5%)
  other arithmetic  48.4 us (5%)
  between operations  16.9 us (2%)
    unnamed x161, local copies, waits for them, and re-layouts  384 us
    psum x1, waiting for transfers between devices, shards(): first_grad = lax.psum(first_part, 'tp')  121 us
    psum x1, waiting for transfers between devices, shards(): second_grad = lax.psum(second_term, 'tp')  119 us
    psum x1, waiting for transfers between devices, shards(): branch = lax.psum(exit_term, 'tp') + exit_bias  109 us
    unnamed x18, waiting for transfers between devices  58.1 us
    reduce_scatter x1, waiting for transfers between devices, shards(): lax.psum_scatter(hidden_weight_grad, ('shard', 'ctx'), scatter_dimension=...  46.2 us
    psum x1, blocking collectives, shards(): lax.psum((first_gain_grad, entry_bias_grad, exit_bias_grad, second_gain_g...  25 us
  transfers between devices with their start and end apart: 14, of which 8 were waited for; matrix products, arithmetic and copies ran while one was open for 30% of the time, Pallas kernels for 0%

commit v1 on v0

v1 whole, which is shorter than its diff:
```python
import functools
import math

import jax
import jax.numpy as jnp
from jax import lax
from jax.experimental import pallas as pl
from jax.experimental.pallas import tpu as pltpu
from jax.sharding import PartitionSpec as P

HDIM = 64
PAIR = 2 * HDIM
EPSILON = 1e-05
MASKED = -1e30
LOW = jnp.bfloat16
SINGLE = jnp.float32


def row_mean(values):
    return jnp.mean(values, -1, keepdims=True)


def dot(left, right):
    return jnp.dot(left, right, preferred_element_type=SINGLE)


def dot_nt(left, right):
    return lax.dot_general(left, right, (((1,), (1,)), ((), ())), preferred_element_type=SINGLE)


def dot_tn(left, right):
    return lax.dot_general(left, right, (((0,), (0,)), ((), ())), preferred_element_type=SINGLE)


def key_positions(meta, block, local, upper):
    base = upper * 2 * local + (meta[1] ^ block) * local
    return base + lax.broadcasted_iota(jnp.int32, (local, 1), 0)


def query_positions(meta, block, local):
    base = meta[0] * 2 * local + (meta[1] ^ block) * local
    return base + lax.broadcasted_iota(jnp.int32, (1, local), 1)


def masks(meta, block, local):
    near_pos = jnp.concatenate([key_positions(meta, b, local, meta[0]) for b in (0, 1)], 0)
    far_pos = jnp.concatenate([key_positions(meta, b, local, 0) for b in (0, 1)], 0)
    near = (near_pos <= query_positions(meta, block, local)) & (near_pos < meta[2])
    far = far_pos < jnp.where(meta[0] == 1, meta[2], 0)
    return near, far


def half_of(values, head):
    lanes = lax.broadcasted_iota(jnp.int32, values.shape, 1)
    return jnp.where((lanes >= HDIM) == (head == 1), values, jnp.zeros_like(values))


def forward_kernel(meta, q_ref, k_ref, v_ref, kf_ref, vf_ref, out_ref, log_ref):
    local = q_ref.shape[0] // 2
    scale = 1.0 / math.sqrt(HDIM)
    for block in (0, 1):
        near, far = masks(meta, block, local)
        rows = pl.ds(block * local, local)
        parts = []
        for head in (0, 1):
            query = half_of(q_ref[rows, :], head) * jnp.asarray(scale, LOW)
            near_s = jnp.where(near, dot_nt(k_ref[...], query), MASKED)
            far_s = jnp.where(far, dot_nt(kf_ref[...], query), MASKED)
            top = jnp.maximum(
                jnp.max(near_s, 0, keepdims=True), jnp.max(far_s, 0, keepdims=True)
            )
            near_p = jnp.exp(near_s - top)
            far_p = jnp.exp(far_s - top)
            total = jnp.sum(near_p, 0, keepdims=True) + jnp.sum(far_p, 0, keepdims=True)
            mixed = dot_tn(v_ref[...], near_p.astype(LOW)) + dot_tn(vf_ref[...], far_p.astype(LOW))
            parts.append(mixed[head * HDIM : (head + 1) * HDIM] / total)
            log_ref[0, head : head + 1, rows] = top + jnp.log(total)
        out_ref[rows, :] = jnp.concatenate(parts, 0).T.astype(LOW)


def attention_forward(meta, queries, near_kv, far_kv):
    rows, width = queries.shape
    pairs = width // PAIR
    block = functools.partial(pl.BlockSpec, (rows, PAIR))
    return pl.pallas_call(
        forward_kernel,
        grid_spec=pltpu.PrefetchScalarGridSpec(
            num_scalar_prefetch=1,
            grid=(pairs,),
            in_specs=[
                block(lambda j, meta: (0, j)),
                block(lambda j, meta: (0, j)),
                block(lambda j, meta: (0, pairs + j)),
                block(lambda j, meta: (0, j)),
                block(lambda j, meta: (0, pairs + j)),
            ],
            out_specs=[
                block(lambda j, meta: (0, j)),
                pl.BlockSpec((1, 2, rows), lambda j, meta: (j, 0, 0)),
            ],
        ),
        out_shape=[
            jax.ShapeDtypeStruct((rows, width), LOW),
            jax.ShapeDtypeStruct((pairs, 2, rows), SINGLE),
        ],
        cost_estimate=pl.CostEstimate(
            flops=8 * rows * rows * width * 2, bytes_accessed=rows * width * 14,
            transcendentals=2 * rows * rows * width // HDIM,
        ),
        name="attend",
    )(meta, queries, near_kv, near_kv, far_kv, far_kv)


def backward_kernel(
    meta, q_ref, k_ref, v_ref, kf_ref, vf_ref, grad_ref, log_ref,
    dq_ref, dk_ref, dv_ref, dkf_ref, dvf_ref, sums
):
    local = q_ref.shape[0] // 2
    scale = 1.0 / math.sqrt(HDIM)
    for block in (0, 1):
        near, far = masks(meta, block, local)
        rows = pl.ds(block * local, local)
        parts = []
        for head in (0, 1):
            query = half_of(q_ref[rows, :], head) * jnp.asarray(scale, LOW)
            out_grad = half_of(grad_ref[rows, :], head)
            log_total = log_ref[0, head : head + 1, rows]
            near_p = jnp.exp(jnp.where(near, dot_nt(k_ref[...], query), MASKED) - log_total)
            far_p = jnp.exp(jnp.where(far, dot_nt(kf_ref[...], query), MASKED) - log_total)
            near_g = dot_nt(v_ref[...], out_grad).astype(LOW).astype(SINGLE)
            far_g = dot_nt(vf_ref[...], out_grad).astype(LOW).astype(SINGLE)
            inner = jnp.sum(near_p * near_g, 0, keepdims=True) + jnp.sum(
                far_p * far_g, 0, keepdims=True
            )
            near_d = (near_p * (near_g - inner)).astype(LOW)
            far_d = (far_p * (far_g - inner)).astype(LOW)
            fresh = (
                dot(near_d, query), dot(near_p.astype(LOW), out_grad),
                dot(far_d, query), dot(far_p.astype(LOW), out_grad),
            )
            for at, value in enumerate(fresh):
                if block == 0 and head == 0:
                    sums[at] = value
                else:
                    sums[at] = sums[at] + value
            mixed = dot_tn(k_ref[...], near_d) + dot_tn(kf_ref[...], far_d)
            parts.append(mixed[head * HDIM : (head + 1) * HDIM] * scale)
        dq_ref[rows, :] = jnp.concatenate(parts, 0).T.astype(LOW)
    dk_ref[...] = sums[0]
    dv_ref[...] = sums[1]
    dkf_ref[...] = sums[2].astype(LOW)
    dvf_ref[...] = sums[3].astype(LOW)


def attention_backward(meta, queries, near_kv, far_kv, grads, logs):
    rows, width = queries.shape
    pairs = width // PAIR
    block = functools.partial(pl.BlockSpec, (rows, PAIR))
    same = lambda j, meta: (0, j)
    return pl.pallas_call(
        backward_kernel,
        grid_spec=pltpu.PrefetchScalarGridSpec(
            num_scalar_prefetch=1,
            grid=(pairs,),
            in_specs=[
                block(same),
                block(same),
                block(lambda j, meta: (0, pairs + j)),
                block(same),
                block(lambda j, meta: (0, pairs + j)),
                block(same),
                pl.BlockSpec((1, 2, rows), lambda j, meta: (j, 0, 0)),
            ],
            out_specs=[block(same)] * 5,
            scratch_shapes=[pltpu.VMEM((4, rows, PAIR), SINGLE)],
        ),
        out_shape=[
            jax.ShapeDtypeStruct((rows, width), LOW),
            jax.ShapeDtypeStruct((rows, width), SINGLE),
            jax.ShapeDtypeStruct((rows, width), SINGLE),
            jax.ShapeDtypeStruct((rows, width), LOW),
            jax.ShapeDtypeStruct((rows, width), LOW),
        ],
        cost_estimate=pl.CostEstimate(
            flops=20 * rows * rows * width * 2, bytes_accessed=rows * width * 30,
            transcendentals=2 * rows * rows * width // HDIM,
        ),
        name="attend_back",
    )(meta, queries, near_kv, near_kv, far_kv, far_kv, grads, logs)


class Place:
    def __init__(self):
        self.n_shard = lax.axis_size("shard")
        self.n_ctx = lax.axis_size("ctx")
        self.n_tp = lax.axis_size("tp")
        self.shard = lax.axis_index("shard")
        ctx = lax.axis_index("ctx")
        self.ctx = ctx
        self.half = ctx // 2
        self.core = ctx % 2
        self.tp = lax.axis_index("tp")
        self.home = self.core == self.tp // 2

    def core_swap(self, value):
        return lax.ppermute(value, "ctx", [(i, i ^ 1) for i in range(self.n_ctx)])

    def half_swap(self, value):
        return lax.ppermute(value, "ctx", [(i, i ^ 2) for i in range(self.n_ctx)])

    def half_up(self, value):
        return lax.ppermute(value, "ctx", [(0, 2), (1, 3)])

    def half_down(self, value):
        return lax.ppermute(value, "ctx", [(2, 0), (3, 1)])

    def shard_swap(self, value):
        return lax.ppermute(value, "shard", [(0, 1), (1, 0)])

    def tp_swap(self, value, mask):
        return lax.ppermute(value, "tp", [(i, i ^ mask) for i in range(self.n_tp)])

    def mixed(self, value, pairs):
        flat = [(a * self.n_tp + b, c * self.n_tp + d) for (a, b), (c, d) in pairs]
        return lax.ppermute(value, ("ctx", "tp"), flat)

    def to_home(self, value):
        return self.mixed(
            value,
            [((2 * h + 1 - z // 2, z), (2 * h + z // 2, z)) for h in (0, 1) for z in range(4)],
        )

    def from_home(self, value):
        return self.mixed(
            value,
            [((2 * h + z // 2, z), (2 * h + 1 - z // 2, z)) for h in (0, 1) for z in range(4)],
        )

    def spread(self, value, mask):
        return self.mixed(
            value,
            [((2 * h + z // 2, z), (2 * h + z // 2, z ^ mask)) for h in (0, 1) for z in range(4)],
        )

    def collect(self, value, mask):
        return self.mixed(
            value,
            [((2 * h + z // 2, z ^ mask), (2 * h + z // 2, z)) for h in (0, 1) for z in range(4)],
        )

    def ordered(self, flag, mine, other):
        first = jnp.where(flag == 0, mine, other)
        second = jnp.where(flag == 0, other, mine)
        return jnp.stack([first, second], 0)

    def over_shards(self, value):
        if self.n_shard == 2:
            return self.ordered(self.shard, value, self.shard_swap(value))
        return lax.all_gather(value, "shard", axis=0)

    def over_halves(self, value):
        return self.ordered(self.half, value, self.half_swap(value))

    def gather(self, piece):
        part, width = piece.shape
        both = self.ordered(self.core, piece, self.to_home(piece)).reshape(2 * part, width)
        near, far, cross = (self.spread(both, mask) for mask in (1, 2, 3))
        first = jnp.where(self.home, both, far)
        second = jnp.where(self.home, near, cross)
        first = self.over_halves(self.over_shards(first))
        first = jnp.moveaxis(first, 0, 1).reshape(-1, width)
        second = self.over_shards(self.over_halves(second)).reshape(-1, width)
        return first, second

    def reduce_halves(self, value, axis):
        sent = lax.dynamic_index_in_dim(value, 1 - self.half, axis, False).astype(LOW)
        kept = lax.dynamic_index_in_dim(value, self.half, axis, False)
        return kept + self.half_swap(sent).astype(SINGLE)

    def reduce_shards(self, value):
        if self.n_shard == 2:
            sent = lax.dynamic_index_in_dim(value, 1 - self.shard, 0, False).astype(LOW)
            kept = lax.dynamic_index_in_dim(value, self.shard, 0, False)
            return kept + self.shard_swap(sent).astype(SINGLE)
        return lax.psum_scatter(value, "shard", scatter_dimension=0, tiled=False)

    def scatter(self, first, second):
        rows, width = first.shape
        shape = (self.n_shard, 2, rows // (2 * self.n_shard), width)
        first = self.reduce_shards(self.reduce_halves(first.reshape(shape), 1))
        second = self.reduce_halves(self.reduce_shards(second.reshape(shape)), 0)
        low_first, low_second = first.astype(LOW), second.astype(LOW)
        near = self.collect(low_second, 1)
        far = self.mixed_far(low_first)
        cross = self.mixed_cross(low_second)
        total = first + near.astype(SINGLE) + far.astype(SINGLE) + cross.astype(SINGLE)
        pieces = total.reshape(2, -1, width)
        sent = lax.dynamic_index_in_dim(pieces, 1 - self.core, 0, False)
        kept = lax.dynamic_index_in_dim(pieces, self.core, 0, False)
        return jnp.where(self.home, kept, self.from_home(sent))

    def mixed_far(self, value):
        return self.collect(value, 2)

    def mixed_cross(self, value):
        return self.collect(value, 3)

    def over_tp(self, value):
        got = [value] + [self.tp_swap(value, mask) for mask in (1, 2, 3)]
        slots = []
        for slot in range(4):
            item = got[3]
            for mask in (0, 1, 2):
                item = jnp.where((self.tp ^ slot) == mask, got[mask], item)
            slots.append(item)
        return jnp.stack(slots, 0)

    def total(self, value):
        value = value + self.core_swap(value)
        value = value + self.half_swap(value)
        value = value + (
            self.shard_swap(value) if self.n_shard == 2 else lax.psum(value, "shard") - value
        )
        value = value + self.tp_swap(value, 1)
        return value + self.tp_swap(value, 2)


def columns(first, second, start, size):
    return jnp.concatenate([first[:, start : start + size], second[:, start : start + size]], 1)


def shards(
    tokens,
    lengths,
    first_gain,
    entry_weight,
    entry_bias,
    exit_weight,
    exit_bias,
    second_gain,
    hidden_weight,
    hidden_bias,
    return_weight,
    return_bias,
    cotangent,
):
    place = Place()
    local, narrow = tokens.shape[1:]
    part = entry_weight.shape[1]
    head_width = entry_weight.shape[2]
    units = hidden_weight.shape[1]

    entry_piece = jnp.moveaxis(entry_weight, 0, 1).reshape(part, 3 * head_width)
    rest_piece = jnp.concatenate([exit_weight.T, hidden_weight, return_weight.T], 1)
    entry_first, entry_second = place.gather(entry_piece)
    rest_first, rest_second = place.gather(rest_piece)
    weight_q = columns(entry_first, entry_second, 0, head_width)
    weight_kv = jnp.concatenate(
        [columns(entry_first, entry_second, at * head_width, head_width) for at in (1, 2)], 1
    )
    exit_t = columns(rest_first, rest_second, 0, head_width)
    hidden_full = columns(rest_first, rest_second, head_width, units)
    return_t = columns(rest_first, rest_second, head_width + units, units)
    biases = jnp.concatenate([entry_bias.reshape(-1), hidden_bias])
    bias_got = [biases] + [place.tp_swap(biases, mask) for mask in (1, 2, 3)]
    bias_first = jnp.where(place.home, bias_got[0], bias_got[2])
    bias_second = jnp.where(place.home, bias_got[1], bias_got[3])
    bias_two = jnp.stack([bias_first, bias_second])
    bias_q = bias_two[:, :head_width].reshape(-1)
    bias_v = bias_two[:, head_width : 2 * head_width].reshape(-1)
    bias_h = bias_two[:, 2 * head_width :].reshape(-1)

    length = lax.dynamic_index_in_dim(lengths, place.tp, 0, False)
    stream_part = lax.dynamic_index_in_dim(tokens, place.tp, 0, False).astype(SINGLE)
    stream = jnp.concatenate([stream_part, -jnp.sum(stream_part, -1, keepdims=True)], 1)
    first_inverse = lax.rsqrt(row_mean(stream * stream) + EPSILON)
    first_unit = stream * first_inverse
    normed_own = (first_unit * first_gain).astype(LOW)
    first_normed = jnp.concatenate([normed_own, place.core_swap(normed_own)], 0)

    position = place.ctx * local + jnp.arange(local, dtype=jnp.int32)
    valid = (position < length).astype(SINGLE)[:, None]
    cot_rows = lax.dynamic_index_in_dim(cotangent, place.tp, 0, False).astype(SINGLE) * valid
    cot_full = jnp.concatenate([cot_rows, jnp.zeros((local, 1), SINGLE)], 1)
    returned_grad_own = (cot_full - row_mean(cot_full)).astype(LOW)
    returned_grad = jnp.concatenate([returned_grad_own, place.core_swap(returned_grad_own)], 0)
    return_bias_grad = jnp.sum(returned_grad_own.astype(SINGLE), 0)

    bias_kv = jnp.concatenate([jnp.zeros_like(bias_v), bias_v])
    near_kv = (dot(first_normed, weight_kv) + bias_kv).astype(LOW)
    far_kv = place.half_up(near_kv)
    queries = (dot(first_normed, weight_q) + bias_q).astype(LOW)
    meta = jnp.stack([place.half, place.core, length]).astype(jnp.int32)
    attended, logs = attention_forward(meta, queries, near_kv, far_kv)

    def joined(partial):
        return partial[:local] + place.core_swap(partial[local:].astype(LOW)).astype(SINGLE)

    branch = joined(dot_nt(attended, exit_t)) + exit_bias
    middle = stream + branch - row_mean(branch)
    second_inverse = lax.rsqrt(row_mean(middle * middle) + EPSILON)
    second_unit = middle * second_inverse
    second_own = (second_unit * second_gain).astype(LOW)
    second_normed = jnp.concatenate([second_own, place.core_swap(second_own)], 0)
    hidden = dot(second_normed, hidden_full) + bias_h
    activated, gelu_pull = jax.vjp(
        lambda values_in: jax.nn.gelu(values_in, approximate=True), hidden
    )
    activated_low = activated.astype(LOW)
    hidden_grad = gelu_pull(dot(returned_grad, return_t))[0].astype(LOW)
    second_grad = joined(dot_nt(hidden_grad, hidden_full))
    returned = joined(dot_nt(activated_low, return_t)) + return_bias
    full_stream = middle + returned - row_mean(returned)
    result = place.over_tp(full_stream.astype(LOW))[:, :, :narrow]

    second_gain_grad = jnp.sum(second_grad * second_unit, 0)
    second_scaled = second_grad * second_gain
    middle_grad = cot_full + second_inverse * (
        second_scaled - second_unit * row_mean(second_scaled * second_unit)
    )
    branch_own = (middle_grad - row_mean(middle_grad)).astype(LOW)
    exit_bias_grad = jnp.sum(branch_own.astype(SINGLE), 0)
    branch_grad = jnp.concatenate([branch_own, place.core_swap(branch_own)], 0)
    attended_grad = dot(branch_grad, exit_t).astype(LOW)
    query_low, near_k, near_v, far_k, far_v = attention_backward(
        meta, queries, near_kv, far_kv, attended_grad, logs
    )
    back_kv = place.half_down(jnp.concatenate([far_k, far_v], 1))
    kv_low = (jnp.concatenate([near_k, near_v], 1) + back_kv.astype(SINGLE)).astype(LOW)
    first_grad = joined(dot_nt(query_low, weight_q) + dot_nt(kv_low, weight_kv))
    first_gain_grad = jnp.sum(first_grad * first_unit, 0)
    first_scaled = first_grad * first_gain
    stream_grad = middle_grad + first_inverse * (
        first_scaled - first_unit * row_mean(first_scaled * first_unit)
    )
    tokens_rows = (stream_grad - stream_grad[:, narrow:]).astype(LOW)
    tokens_grad = place.over_tp(tokens_rows)[:, :, :narrow]

    hidden_weight_grad = dot_tn(second_normed, hidden_grad)
    return_weight_grad = dot_tn(returned_grad, activated_low)
    mlp = place.scatter(
        *(
            jnp.concatenate(
                [hidden_weight_grad[:, cut], return_weight_grad[:, cut]], 1
            )
            for cut in (slice(0, units), slice(units, None))
        )
    )
    query_weight_grad = dot_tn(first_normed, query_low)
    kv_weight_grad = dot_tn(first_normed, kv_low)
    exit_weight_grad = dot_tn(branch_grad, attended)
    width = 2 * head_width
    heads = place.scatter(
        *(
            jnp.concatenate(
                [
                    query_weight_grad[:, at : at + head_width],
                    kv_weight_grad[:, at : at + head_width],
                    kv_weight_grad[:, width + at : width + at + head_width],
                    exit_weight_grad[:, at : at + head_width],
                ],
                1,
            )
            for at in (0, head_width)
        )
    )
    entry_grad = jnp.moveaxis(heads[:, : 3 * head_width].reshape(part, 3, head_width), 1, 0)
    exit_grad = heads[:, 3 * head_width :].T
    hidden_out = mlp[:, :units]
    return_out = mlp[:, units:].T

    query_sum = jnp.sum(query_low.astype(SINGLE), 0).reshape(2, head_width)
    value_sum = jnp.sum(kv_low[:, width:].astype(SINGLE), 0).reshape(2, head_width)
    hidden_sum = jnp.sum(hidden_grad.astype(SINGLE), 0).reshape(2, units)
    blocks = jnp.concatenate([query_sum, value_sum, hidden_sum], 1)
    first_id = jnp.where(place.home, place.tp, place.tp ^ 2)
    slots = []
    for slot in range(4):
        slots.append(
            jnp.where(first_id == slot, blocks[0], 0.0)
            + jnp.where(first_id == (slot ^ 1), blocks[1], 0.0)
        )
    vectors = jnp.concatenate(
        [first_gain_grad, exit_bias_grad, second_gain_grad, return_bias_grad] + slots
    )
    vectors = place.total(vectors)
    wide = narrow + 1
    mine = lax.dynamic_index_in_dim(vectors[4 * wide :].reshape(4, -1), place.tp, 0, False)
    return (
        result,
        tokens_grad,
        vectors[:wide],
        entry_grad,
        mine[:width].reshape(2, head_width),
        exit_grad,
        vectors[wide : 2 * wide],
        vectors[2 * wide : 3 * wide],
        hidden_out,
        mine[width:],
        return_out,
        vectors[3 * wide : 4 * wide],
    )


def solution(mesh):
    return jax.shard_map(
        shards,
        mesh=mesh,
        in_specs=(
            P("shard", "ctx", None),
            P("shard"),
            P(),
            P(None, ("shard", "ctx"), "tp"),
            P(None, "tp"),
            P("tp", ("shard", "ctx")),
            P(),
            P(),
            P(("shard", "ctx"), "tp"),
            P("tp"),
            P("tp", ("shard", "ctx")),
            P(),
            P("shard", "ctx", None),
        ),
        out_specs=(
            P("shard", "ctx", None),
            P("shard", "ctx", None),
            P(),
            P(None, ("shard", "ctx"), "tp"),
            P(None, "tp"),
            P("tp", ("shard", "ctx")),
            P(),
            P(),
            P(("shard", "ctx"), "tp"),
            P("tp"),
            P("tp", ("shard", "ctx")),
            P(),
        ),
        check_vma=False,
    )
```

time: 1070 us -> 389 us (0.36)
  local copies, waits for them, and re-layouts: 400 us -> 52.3 us
  waiting for transfers between devices: 473 us -> 129 us
  starting transfers between devices: 1.86 us -> 96.1 us
  blocking collectives: 50.5 us -> 0 us
  matrix products: 69.6 us -> 31.8 us
  Pallas kernels: 0 us -> 24.3 us
  between operations: 16.9 us -> 2.55 us
    unnamed x161 -> x151, local copies, waits for them, and re-layouts: 384 us -> 13.5 us
    psum x4 -> x0, waiting for transfers between devices: 350 us -> none  [the longest x1 121 us: shards(): first_grad = lax.psum(first_part, 'tp')]
    ppermute x0 -> x56, waiting for transfers between devices: none -> 129 us  [the longest x16 41.2 us: mixed(): return lax.ppermute(value, ('ctx', 'tp'), flat)]
    ppermute x0 -> x56, starting transfers between devices: none -> 96.1 us  [the longest x16 35.3 us: mixed(): return lax.ppermute(value, ('ctx', 'tp'), flat)]
    unnamed x18 -> x0, waiting for transfers between devices: 58.1 us -> none
    reduce_scatter x2 -> x0, waiting for transfers between devices: 58 us -> none  [the longest x1 46.2 us: shards(): lax.psum_scatter(hidden_weight_grad, ('shard', 'ctx'), scatter_dimension=...]
    dot_general x23 -> x15, matrix products: 68 us -> 31.8 us  [the longest x5 14.8 us: dot(): return jnp.dot(left, right, preferred_element_type=SINGLE)]
    all_gather x2 -> x0, blocking collectives: 25.5 us -> none  [the longest x1 13.1 us: shards(): lax.all_gather(entry_weight, ('shard', 'ctx'), axis=1, tiled=True)]
  transfers between devices with their start and end apart: 14 -> 56, of which waited for: 8 -> 21; matrix products, arithmetic and copies ran while one was open for 30% -> 29% of each run, Pallas kernels for 0% -> 6%
where the time goes in v1:
time: 389 us; the launch traced here: 381 us
  waiting for transfers between devices  129 us (33%)
  starting transfers between devices  96.1 us (25%)
  local copies, waits for them, and re-layouts  52.3 us (13%)
  other arithmetic  44.4 us (11%)
  matrix products  31.8 us (8%)
  Pallas kernels  24.3 us (6%)
    ppermute x16, waiting for transfers between devices, mixed(): return lax.ppermute(value, ('ctx', 'tp'), flat)  41.2 us
    ppermute x9, waiting for transfers between devices, half_swap(): return lax.ppermute(value, 'ctx', [(i, i ^ 2) for i in range(self.n_ctx)])  36.5 us
    ppermute x16, starting transfers between devices, mixed(): return lax.ppermute(value, ('ctx', 'tp'), flat)  35.3 us
    ppermute x11, waiting for transfers between devices, tp_swap(): return lax.ppermute(value, 'tp', [(i, i ^ mask) for i in range(self.n_tp)])  29.3 us
    ppermute x11, starting transfers between devices, tp_swap(): return lax.ppermute(value, 'tp', [(i, i ^ mask) for i in range(self.n_tp)])  29.1 us
    dot_general x5, matrix products, dot(): return jnp.dot(left, right, preferred_element_type=SINGLE)  14.8 us
    pallas_call x1, Pallas kernels, attention_backward(): pl.pallas_call(backward_kernel, grid_spec=pltpu.PrefetchScalarGridSpec(nu...  13.8 us
    unnamed x151, local copies, waits for them, and re-layouts  13.5 us
  transfers between devices with their start and end apart: 56, of which 21 were waited for; matrix products, arithmetic and copies ran while one was open for 29% of the time, Pallas kernels for 6%

profile of v1, /device:TPU:0, one launch (start us, length us, event | category | flops | bytes accessed | tf_op | source)
XLA Modules:
  0.0 380.9 jit_solution(2053086662211609656)
XLA Ops:
  2.1 3.1 collective-permute-start.10
  5.2 2.5 collective-permute-start.11
  10.1 3.5 constant_dynamic-slice_fusion.1
  22.3 5.5 %collective-permute-start.2 = (bf16[192,576]{1,0:T(8,128)(2,1)S(1)}, bf16[192,576]{1,0:T(8,128)(2,1)S(1)}, u32[]{:S(2)}, u32[]{:S(2)}) collective-permute-start(bf16[192,576]{1,0:T(8,128)(2,1)S(1)} %bitcast.186), channel_id=1, source_target_pairs={{0,2},{1,3},{6,4},{7,5},{8,10},{9,11},{14,12},{15,13},{16,18},{17,... | collective-permute-start | bytes 663560 | tf_op jit(solution)/shard_map/ppermute | solution.py:225
  27.8 2.6 collective-permute-start.5
  32.8 3.3 collective-permute-start.17
  36.1 3.5 collective-permute-start.18
  42.7 4.7 %collective-permute-done.3 = bf16[192,576]{1,0:T(8,128)(2,1)S(1)} collective-permute-done((bf16[192,576]{1,0:T(8,128)(2,1)S(1)}, bf16[192,576]{1,0:T(8,128)(2,1)S(1)}, u32[]{:S(2)}, u32[]{:S(2)}) %collective-permute-start.3) | collective-permute-done | bytes 221216 | tf_op jit(solution)/shard_map/ppermute | solution.py:218
  49.1 6.2 %collective-permute-done.7 = bf16[192,576]{1,0:T(8,128)(2,1)S(1)} collective-permute-done((bf16[192,576]{1,0:T(8,128)(2,1)S(1)}, bf16[192,576]{1,0:T(8,128)(2,1)S(1)}, u32[]{:S(2)}, u32[]{:S(2)}) %collective-permute-start.7) | collective-permute-done | bytes 221216 | tf_op jit(solution)/shard_map/ppermute | solution.py:209
  61.0 8.4 %collective-permute-done.4 = bf16[2,192,576]{2,1,0:T(8,128)(2,1)S(1)} collective-permute-done((bf16[2,192,576]{2,1,0:T(8,128)(2,1)S(1)}, bf16[2,192,576]{2,1,0:T(8,128)(2,1)S(1)}, u32[]{:S(2)}, u32[]{:S(2)}) %collective-permute-start.4) | collective-permute-done | bytes 442400 | tf_op jit(solution)/shard_map/ppermute | solution.py:209
  71.4 7.5 %collective-permute-done.19 = bf16[192,1728]{1,0:T(8,128)(2,1)S(1)} collective-permute-done((bf16[192,1728]{1,0:T(8,128)(2,1)S(1)}, bf16[192,1728]{1,0:T(8,128)(2,1)S(1)}, u32[]{:S(2)}, u32[]{:S(2)}) %collective-permute-start.19) | collective-permute-done | bytes 663584 | tf_op jit(solution)/shard_map/ppermute | solution.py:209
  81.7 2.9 add_convert_fusion.k_ref.v_ref
  84.6 4.4 %collective-permute-start.12 = (bf16[512,768]{1,0:T(8,128)(2,1)}, bf16[512,768]{1,0:T(8,128)(2,1)}, u32[]{:S(2)}, u32[]{:S(2)}) collective-permute-start(bf16[512,768]{1,0:T(8,128)(2,1)} %add_convert_fusion.k_ref.v_ref), channel_id=1, source_target_pairs={{0,8},{4,12},{1,9},{5,13},{2,10},{6,14},{3,11},{7,15},{16,24},{20,... | collective-permute-start | bytes 2359304 | tf_op jit(solution)/shard_map/ppermute | solution.py:212
  92.6 2.8 fusion.11.q_ref
  95.3 10.9 %collective-permute-done.12.kf_ref.vf_ref = bf16[512,768]{1,0:T(8,128)(2,1)} collective-permute-done((bf16[512,768]{1,0:T(8,128)(2,1)}, bf16[512,768]{1,0:T(8,128)(2,1)}, u32[]{:S(2)}, u32[]{:S(2)}) %collective-permute-start.12) | collective-permute-done | bytes 786464 | tf_op jit(solution)/shard_map/ppermute | solution.py:212
  106.3 10.5 %attend.1 = (bf16[512,384]{1,0:T(8,128)(2,1)}, f32[3,2,512]{2,1,0:T(2,128)}) custom-call(s32[3]{0:T(128)} %pad_add_fusion.meta, bf16[512,384]{1,0:T(8,128)(2,1)} %fusion.11.q_ref, bf16[512,768]{1,0:T(8,128)(2,1)} %add_convert_fusion.k_ref.v_ref, bf16[512,768]{1,0:T(8,128)(2,1)} %add_convert_fusion.k_ref.v_ref, ...), custom_call_target="tpu_custom_call" | custom-call | flops 1610612736 | bytes 2752512 | tf_op jit(solution)/shard_map/attend/pallas_call | solution.py:85
  118.7 10.7 %collective-permute-done.16 = bf16[2,192,1728]{2,1,0:T(8,128)(2,1)} collective-permute-done((bf16[2,192,1728]{2,1,0:T(8,128)(2,1)}, bf16[2,192,1728]{2,1,0:T(8,128)(2,1)}, u32[]{:S(2)}, u32[]{:S(2)}) %collective-permute-start.16) | collective-permute-done | bytes 1327136 | tf_op jit(solution)/shard_map/ppermute | solution.py:209
  139.8 4.4 %fusion.60 = (bf16[768,768]{1,0:T(8,128)(2,1)S(1)}, bf16[768,768]{1,0:T(8,128)(2,1)S(1)}, bf16[768,768]{1,0:T(8,128)(2,1)S(1)}, bf16[768,768]{1,0:T(8,128)(2,1)S(1)}) fusion(bf16[768,1728]{1,0:T(8,128)(2,1)} %bitcast.171, bf16[768,1728]{1,0:T(8,128)(2,1)S(1)} %bitcast.169), kind=kLoop, calls=%fused_computation.226 | loop fusion | bytes 9437184 | tf_op jit(solution)/shard_map/slice | solution.py:329
  147.7 5.2 %convert_reduce_fusion = (f32[1536]{0:T(1024)S(1)}, bf16[512,1536]{1,0:T(8,128)(2,1)S(1)}) fusion(f32[512,1536]{1,0:T(8,128)S(1)} %convolution_add_fusion, bf16[768,768]{1,0:T(8,128)(2,1)S(1)} %get-tuple-element.156, bf16[768,768]{1,0:T(8,128)(2,1)S(1)} %get-tuple-element.95, bf16[256,768]{1,0:T(8,128)(2,1)} %collective-permute-done.27, ...), kind=kOutput, calls=%fused_computation.12 | convolution fusion | flops 1231550976 | bytes 7870464 | tf_op jit(solution)/shard_map/dot_general | solution.py:24
  156.6 3.7 fusion.24
  168.8 2.5 collective-permute-start.48
  172.4 4.7 %collective-permute-start.24 = (bf16[256,768]{1,0:T(8,128)(2,1)S(1)}, bf16[256,768]{1,0:T(8,128)(2,1)S(1)}, u32[]{:S(2)}, u32[]{:S(2)}) collective-permute-start(bf16[256,768]{1,0:T(8,128)(2,1)S(1)} %get-tuple-element.132), channel_id=1, source_target_pairs={{0,2},{1,3},{2,0},{3,1},{4,6},{5,7},{6,4},{7,5},{8,10},{9,11},{10,... | collective-permute-start | bytes 1179656 | tf_op jit(solution)/shard_map/ppermute | solution.py:221
  177.1 6.8 %collective-permute-start.25 = (bf16[256,768]{1,0:T(8,128)(2,1)S(1)}, bf16[256,768]{1,0:T(8,128)(2,1)S(1)}, u32[]{:S(2)}, u32[]{:S(2)}) collective-permute-start(bf16[256,768]{1,0:T(8,128)(2,1)S(1)} %get-tuple-element.132), channel_id=1, source_target_pairs={{0,1},{1,0},{2,3},{3,2},{4,5},{5,4},{6,7},{7,6},{8,9},{9,8},{10,11... | collective-permute-start | bytes 1179656 | tf_op jit(solution)/shard_map/ppermute | solution.py:221
  184.1 11.4 %collective-permute-done.24 = bf16[256,768]{1,0:T(8,128)(2,1)S(1)} collective-permute-done((bf16[256,768]{1,0:T(8,128)(2,1)S(1)}, bf16[256,768]{1,0:T(8,128)(2,1)S(1)}, u32[]{:S(2)}, u32[]{:S(2)}) %collective-permute-start.24) | collective-permute-done | bytes 393248 | tf_op jit(solution)/shard_map/ppermute | solution.py:221
  195.5 14.3 %collective-permute-done.26 = bf16[256,768]{1,0:T(8,128)(2,1)S(1)} collective-permute-done((bf16[256,768]{1,0:T(8,128)(2,1)S(1)}, bf16[256,768]{1,0:T(8,128)(2,1)S(1)}, u32[]{:S(2)}, u32[]{:S(2)}) %collective-permute-start.26) | collective-permute-done | bytes 393248 | tf_op jit(solution)/shard_map/ppermute | solution.py:221
  210.3 2.2 copy.76
  212.5 2.5 convolution_convert_fusion.grad_ref
  215.0 13.8 %attend_back.1 = (bf16[512,384]{1,0:T(8,128)(2,1)}, f32[512,384]{1,0:T(8,128)}, f32[512,384]{1,0:T(8,128)}, bf16[512,384]{1,0:T(8,128)(2,1)}, bf16[512,384]{1,0:T(8,128)(2,1)}) custom-call(s32[3]{0:T(128)} %pad_add_fusion.meta, bf16[512,384]{1,0:T(8,128)(2,1)} %fusion.11.q_ref, bf16[512,768]{1,0:T(8,128)(2,1)} %add_convert_fusion.k_ref.v_ref, ...), custom_call_target="tpu_custom_call" | custom-call | flops 4026531840 | bytes 5898240 | tf_op jit(solution)/shard_map/attend_back/pallas_call | solution.py:160
  228.8 2.1 pad_maximum_fusion.29
  237.7 2.9 bitcast_add_fusion
  241.6 3.5 collective-permute-start.51
  248.3 5.3 %collective-permute-done.30 = bf16[512,768]{1,0:T(8,128)(2,1)} collective-permute-done((bf16[512,768]{1,0:T(8,128)(2,1)}, bf16[512,768]{1,0:T(8,128)(2,1)}, u32[]{:S(2)}, u32[]{:S(2)}) %collective-permute-start.30) | collective-permute-done | bytes 786464 | tf_op jit(solution)/shard_map/ppermute | solution.py:215
  265.5 2.2 fusion.19
  269.7 2.0 copy.72
  271.8 2.2 fusion.18
  274.1 2.6 fusion.14
  278.0 4.7 %collective-permute-start.52 = (bf16[192,1536]{1,0:T(8,128)(2,1)}, bf16[192,1536]{1,0:T(8,128)(2,1)}, u32[]{:S(2)}, u32[]{:S(2)}) collective-permute-start(bf16[192,1536]{1,0:T(8,128)(2,1)} %fusion.14), channel_id=1, source_target_pairs={{1,0},{0,1},{7,6},{6,7},{9,8},{8,9},{15,14},{14,15},{17,16},{16,17... | collective-permute-start | bytes 1769480 | tf_op jit(solution)/shard_map/ppermute | solution.py:225
  284.5 2.0 fusion.17
  286.5 2.1 collective-permute-start.36
  288.6 2.0 collective-permute-done.36
  294.6 3.3 collective-permute-start.38
  299.7 3.3 collective-permute-start.39
  308.4 3.6 collective-permute-start.32
  316.7 30.1 %collective-permute-done.53 = bf16[192,1536]{1,0:T(8,128)(2,1)S(1)} collective-permute-done((bf16[192,1536]{1,0:T(8,128)(2,1)}, bf16[192,1536]{1,0:T(8,128)(2,1)S(1)}, u32[]{:S(2)}, u32[]{:S(2)}) %collective-permute-start.53) | collective-permute-done | bytes 589856 | tf_op jit(solution)/shard_map/ppermute | solution.py:225
  353.5 2.1 collective-permute-start.55
  362.1 2.2 copy.77
  364.3 5.5 %collective-permute-done.46 = bf16[192,768]{1,0:T(8,128)(2,1)} collective-permute-done((bf16[192,768]{1,0:T(8,128)(2,1)}, bf16[192,768]{1,0:T(8,128)(2,1)}, u32[]{:S(2)}, u32[]{:S(2)}) %collective-permute-start.46) | collective-permute-done | bytes 294944 | tf_op jit(solution)/shard_map/ppermute | solution.py:225
  369.8 5.2 %collective-permute-done.45 = bf16[192,768]{1,0:T(8,128)(2,1)} collective-permute-done((bf16[192,768]{1,0:T(8,128)(2,1)}, bf16[192,768]{1,0:T(8,128)(2,1)}, u32[]{:S(2)}, u32[]{:S(2)}) %collective-permute-start.45) | collective-permute-done | bytes 294944 | tf_op jit(solution)/shard_map/ppermute | solution.py:225
  (377 shorter events, 125.1 us)
Async XLA Ops:
  2.1 18.4 %collective-permute-start.10 = (f32[1152]{0:T(1024)S(1)}, f32[1152]{0:T(1024)S(1)}, u32[]{:S(2)}, u32[]{:S(2)}) collective-permute-start(f32[1152]{0:T(1024)S(1)} %constant_dynamic-update-slice_fusion.9), channel_id=1, source_target_pairs={{0,1},{1,0},{2,3},{3,2},{4,5},{5,4},{6,7},{7,6},{8,9},{9,8},{10,11... | collective-permute-start | bytes 13832 | tf_op jit(solution)/shard_map/ppermute | solution.py:221
  5.2 16.6 %collective-permute-start.11 = (f32[1152]{0:T(1024)S(1)}, f32[1152]{0:T(1024)S(1)}, u32[]{:S(2)}, u32[]{:S(2)}) collective-permute-start(f32[1152]{0:T(1024)S(1)} %constant_dynamic-update-slice_fusion.9), channel_id=1, source_target_pairs={{0,3},{1,2},{2,1},{3,0},{4,7},{5,6},{6,5},{7,4},{8,11},{9,10},{10,... | collective-permute-start | bytes 13832 | tf_op jit(solution)/shard_map/ppermute | solution.py:221
  7.6 14.2 %collective-permute-start.9 = (f32[1152]{0:T(1024)S(1)}, f32[1152]{0:T(1024)S(1)}, u32[]{:S(2)}, u32[]{:S(2)}) collective-permute-start(f32[1152]{0:T(1024)S(1)} %constant_dynamic-update-slice_fusion.9), channel_id=1, source_target_pairs={{0,2},{1,3},{2,0},{3,1},{4,6},{5,7},{6,4},{7,5},{8,10},{9,11},{10,... | collective-permute-start | bytes 13832 | tf_op jit(solution)/shard_map/ppermute | solution.py:221
  8.8 13.2 %collective-permute-start.1 = (bf16[96,576]{0,1:T(8,128)(2,1)S(1)}, bf16[96,576]{0,1:T(8,128)(2,1)S(1)}, u32[]{:S(2)}, u32[]{:S(2)}) collective-permute-start(bf16[96,576]{0,1:T(8,128)(2,1)S(1)} %bitcast.189), channel_id=1, source_target_pairs={{4,0},{5,1},{2,6},{3,7},{12,8},{13,9},{10,14},{11,15},{20,16},{21,... | collective-permute-start | bytes 331784 | tf_op jit(solution)/shard_map/ppermute | solution.py:225
  16.3 65.4 %collective-permute-start = (bf16[256,768]{1,0:T(8,128)(2,1)}, bf16[256,768]{1,0:T(8,128)(2,1)}, u32[]{:S(2)}, u32[]{:S(2)}) collective-permute-start(bf16[256,768]{1,0:T(8,128)(2,1)} %multiply_convert_fusion.2), channel_id=1, source_target_pairs={{0,4},{4,0},{8,12},{12,8},{1,5},{5,1},{9,13},{13,9},{2,6},{6,2},{1... | collective-permute-start | bytes 1179656 | tf_op jit(solution)/shard_map/ppermute | solution.py:206
  20.5 11.2 %collective-permute-start.13 = (bf16[96,1728]{1,0:T(8,128)(2,1)S(1)}, bf16[96,1728]{1,0:T(8,128)(2,1)}, u32[]{:S(2)}, u32[]{:S(2)}) collective-permute-start(bf16[96,1728]{1,0:T(8,128)(2,1)S(1)} %concatenate.72), channel_id=1, source_target_pairs={{4,0},{5,1},{2,6},{3,7},{12,8},{13,9},{10,14},{11,15},{20,16},{21,... | collective-permute-start | bytes 995336 | tf_op jit(solution)/shard_map/ppermute | solution.py:225
  22.3 13.8 %collective-permute-start.2 = (bf16[192,576]{1,0:T(8,128)(2,1)S(1)}, bf16[192,576]{1,0:T(8,128)(2,1)S(1)}, u32[]{:S(2)}, u32[]{:S(2)}) collective-permute-start(bf16[192,576]{1,0:T(8,128)(2,1)S(1)} %bitcast.186), channel_id=1, source_target_pairs={{0,2},{1,3},{6,4},{7,5},{8,10},{9,11},{14,12},{15,13},{16,18},{17,... | collective-permute-start | bytes 663560 | tf_op jit(solution)/shard_map/ppermute | solution.py:225
  27.8 12.0 %collective-permute-start.5 = (bf16[192,576]{1,0:T(8,128)(2,1)S(1)}, bf16[192,576]{1,0:T(8,128)(2,1)S(1)}, u32[]{:S(2)}, u32[]{:S(2)}) collective-permute-start(bf16[192,576]{1,0:T(8,128)(2,1)S(1)} %bitcast.187), channel_id=1, source_target_pairs={{0,1},{1,0},{6,7},{7,6},{8,9},{9,8},{14,15},{15,14},{16,17},{17,16... | collective-permute-start | bytes 663560 | tf_op jit(solution)/shard_map/ppermute | solution.py:225
  30.4 10.8 %collective-permute-start.6 = (bf16[192,576]{1,0:T(8,128)(2,1)S(1)}, bf16[192,576]{1,0:T(8,128)(2,1)S(1)}, u32[]{:S(2)}, u32[]{:S(2)}) collective-permute-start(bf16[192,576]{1,0:T(8,128)(2,1)S(1)} %bitcast.188), channel_id=1, source_target_pairs={{0,3},{1,2},{6,5},{7,4},{8,11},{9,10},{14,13},{15,12},{16,19},{17,... | collective-permute-start | bytes 663560 | tf_op jit(solution)/shard_map/ppermute | solution.py:225
  32.8 24.1 %collective-permute-start.17 = (bf16[192,1728]{1,0:T(8,128)(2,1)S(1)}, bf16[192,1728]{1,0:T(8,128)(2,1)S(1)}, u32[]{:S(2)}, u32[]{:S(2)}) collective-permute-start(bf16[192,1728]{1,0:T(8,128)(2,1)S(1)} %bitcast.180), channel_id=1, source_target_pairs={{0,1},{1,0},{6,7},{7,6},{8,9},{9,8},{14,15},{15,14},{16,17},{17,16... | collective-permute-start | bytes 1990664 | tf_op jit(solution)/shard_map/ppermute | solution.py:225
  36.1 22.4 %collective-permute-start.18 = (bf16[192,1728]{1,0:T(8,128)(2,1)S(1)}, bf16[192,1728]{1,0:T(8,128)(2,1)S(1)}, u32[]{:S(2)}, u32[]{:S(2)}) collective-permute-start(bf16[192,1728]{1,0:T(8,128)(2,1)S(1)} %bitcast.181), channel_id=1, source_target_pairs={{0,3},{1,2},{6,5},{7,4},{8,11},{9,10},{14,13},{15,12},{16,19},{17,... | collective-permute-start | bytes 1990664 | tf_op jit(solution)/shard_map/ppermute | solution.py:225
  39.8 19.5 %collective-permute-start.14 = (bf16[192,1728]{1,0:T(8,128)(2,1)S(1)}, bf16[192,1728]{1,0:T(8,128)(2,1)S(1)}, u32[]{:S(2)}, u32[]{:S(2)}) collective-permute-start(bf16[192,1728]{1,0:T(8,128)(2,1)S(1)} %bitcast.182), channel_id=1, source_target_pairs={{0,2},{1,3},{6,4},{7,5},{8,10},{9,11},{14,12},{15,13},{16,18},{17,... | collective-permute-start | bytes 1990664 | tf_op jit(solution)/shard_map/ppermute | solution.py:225
  41.2 6.3 %collective-permute-start.3 = (bf16[192,576]{1,0:T(8,128)(2,1)S(1)}, bf16[192,576]{1,0:T(8,128)(2,1)S(1)}, u32[]{:S(2)}, u32[]{:S(2)}) collective-permute-start(bf16[192,576]{1,0:T(8,128)(2,1)S(1)} %broadcast_select_fusion.3), channel_id=1, source_target_pairs={{0,16},{16,0},{1,17},{17,1},{2,18},{18,2},{3,19},{19,3},{4,20},{20... | collective-permute-start | bytes 663560 | tf_op jit(solution)/shard_map/ppermute | solution.py:218
  47.4 7.9 %collective-permute-start.7 = (bf16[192,576]{1,0:T(8,128)(2,1)S(1)}, bf16[192,576]{1,0:T(8,128)(2,1)S(1)}, u32[]{:S(2)}, u32[]{:S(2)}) collective-permute-start(bf16[192,576]{1,0:T(8,128)(2,1)S(1)} %broadcast_select_fusion.2), channel_id=1, source_target_pairs={{0,8},{4,12},{8,0},{12,4},{1,9},{5,13},{9,1},{13,5},{2,10},{6,14},... | collective-permute-start | bytes 663560 | tf_op jit(solution)/shard_map/ppermute | solution.py:209
  55.3 14.1 %collective-permute-start.4 = (bf16[2,192,576]{2,1,0:T(8,128)(2,1)S(1)}, bf16[2,192,576]{2,1,0:T(8,128)(2,1)S(1)}, u32[]{:S(2)}, u32[]{:S(2)}) collective-permute-start(bf16[2,192,576]{2,1,0:T(8,128)(2,1)S(1)} %pad_maximum_fusion.39), channel_id=1, source_target_pairs={{0,8},{4,12},{8,0},{12,4},{1,9},{5,13},{9,1},{13,5},{2,10},{6,14},... | collective-permute-start | bytes 1327112 | tf_op jit(solution)/shard_map/ppermute | solution.py:209
  57.0 12.8 %collective-permute-start.8 = (bf16[2,192,576]{2,1,0:T(8,128)(2,1)S(1)}, bf16[2,192,576]{2,1,0:T(8,128)(2,1)S(1)}, u32[]{:S(2)}, u32[]{:S(2)}) collective-permute-start(bf16[2,192,576]{2,1,0:T(8,128)(2,1)S(1)} %pad_maximum_fusion.40), channel_id=1, source_target_pairs={{0,16},{16,0},{1,17},{17,1},{2,18},{18,2},{3,19},{19,3},{4,20},{20... | collective-permute-start | bytes 1327112 | tf_op jit(solution)/shard_map/ppermute | solution.py:218
  58.6 20.3 %collective-permute-start.19 = (bf16[192,1728]{1,0:T(8,128)(2,1)S(1)}, bf16[192,1728]{1,0:T(8,128)(2,1)S(1)}, u32[]{:S(2)}, u32[]{:S(2)}) collective-permute-start(bf16[192,1728]{1,0:T(8,128)(2,1)S(1)} %broadcast_select_fusion), channel_id=1, source_target_pairs={{0,8},{4,12},{8,0},{12,4},{1,9},{5,13},{9,1},{13,5},{2,10},{6,14},... | collective-permute-start | bytes 1990664 | tf_op jit(solution)/shard_map/ppermute | solution.py:209
  59.4 29.7 %collective-permute-start.15 = (bf16[192,1728]{1,0:T(8,128)(2,1)S(1)}, bf16[192,1728]{1,0:T(8,128)(2,1)S(1)}, u32[]{:S(2)}, u32[]{:S(2)}) collective-permute-start(bf16[192,1728]{1,0:T(8,128)(2,1)S(1)} %broadcast_select_fusion.1), channel_id=1, source_target_pairs={{0,16},{16,0},{1,17},{17,1},{2,18},{18,2},{3,19},{19,3},{4,20},{20... | collective-permute-start | bytes 1990664 | tf_op jit(solution)/shard_map/ppermute | solution.py:218
  80.2 36.6 %collective-permute-start.20 = (bf16[2,192,1728]{2,1,0:T(8,128)(2,1)}, bf16[2,192,1728]{2,1,0:T(8,128)(2,1)}, u32[]{:S(2)}, u32[]{:S(2)}) collective-permute-start(bf16[2,192,1728]{2,1,0:T(8,128)(2,1)} %pad_maximum_fusion.21), channel_id=1, source_target_pairs={{0,16},{16,0},{1,17},{17,1},{2,18},{18,2},{3,19},{19,3},{4,20},{20... | collective-permute-start | bytes 3981320 | tf_op jit(solution)/shard_map/ppermute | solution.py:218
  84.6 21.6 %collective-permute-start.12 = (bf16[512,768]{1,0:T(8,128)(2,1)}, bf16[512,768]{1,0:T(8,128)(2,1)}, u32[]{:S(2)}, u32[]{:S(2)}) collective-permute-start(bf16[512,768]{1,0:T(8,128)(2,1)} %add_convert_fusion.k_ref.v_ref), channel_id=1, source_target_pairs={{0,8},{4,12},{1,9},{5,13},{2,10},{6,14},{3,11},{7,15},{16,24},{20,... | collective-permute-start | bytes 2359304 | tf_op jit(solution)/shard_map/ppermute | solution.py:212
  91.3 38.1 %collective-permute-start.16 = (bf16[2,192,1728]{2,1,0:T(8,128)(2,1)}, bf16[2,192,1728]{2,1,0:T(8,128)(2,1)}, u32[]{:S(2)}, u32[]{:S(2)}) collective-permute-start(bf16[2,192,1728]{2,1,0:T(8,128)(2,1)} %pad_maximum_fusion.20), channel_id=1, source_target_pairs={{0,8},{4,12},{8,0},{12,4},{1,9},{5,13},{9,1},{13,5},{2,10},{6,14},... | collective-permute-start | bytes 3981320 | tf_op jit(solution)/shard_map/ppermute | solution.py:209
  135.3 12.4 %collective-permute-start.27 = (bf16[256,768]{1,0:T(8,128)(2,1)}, bf16[256,768]{1,0:T(8,128)(2,1)}, u32[]{:S(2)}, u32[]{:S(2)}) collective-permute-start(bf16[256,768]{1,0:T(8,128)(2,1)} %get-tuple-element.83), channel_id=1, source_target_pairs={{0,4},{4,0},{8,12},{12,8},{1,5},{5,1},{9,13},{13,9},{2,6},{6,2},{1... | collective-permute-start | bytes 1179656 | tf_op jit(solution)/shard_map/ppermute | solution.py:206
  155.2 16.1 %collective-permute-start.28 = (bf16[256,768]{1,0:T(8,128)(2,1)}, bf16[256,768]{1,0:T(8,128)(2,1)S(1)}, u32[]{:S(2)}, u32[]{:S(2)}) collective-permute-start(bf16[256,768]{1,0:T(8,128)(2,1)} %slice.313), channel_id=1, source_target_pairs={{0,4},{4,0},{8,12},{12,8},{1,5},{5,1},{9,13},{13,9},{2,6},{6,2},{1... | collective-permute-start | bytes 1179656 | tf_op jit(solution)/shard_map/ppermute | solution.py:206
  156.4 15.3 %collective-permute-start.23 = (bf16[256,768]{1,0:T(8,128)(2,1)}, bf16[256,768]{1,0:T(8,128)(2,1)S(1)}, u32[]{:S(2)}, u32[]{:S(2)}) collective-permute-start(bf16[256,768]{1,0:T(8,128)(2,1)} %slice.314), channel_id=1, source_target_pairs={{0,4},{4,0},{8,12},{12,8},{1,5},{5,1},{9,13},{13,9},{2,6},{6,2},{1... | collective-permute-start | bytes 1179656 | tf_op jit(solution)/shard_map/ppermute | solution.py:206
  165.6 72.1 %collective-permute-start.50 = (bf16[2,192,1536]{2,1,0:T(8,128)(2,1)}, bf16[2,192,1536]{2,1,0:T(8,128)(2,1)}, u32[]{:S(2)}, u32[]{:S(2)}) collective-permute-start(bf16[2,192,1536]{2,1,0:T(8,128)(2,1)} %fusion.12), channel_id=1, source_target_pairs={{0,16},{16,0},{1,17},{17,1},{2,18},{18,2},{3,19},{19,3},{4,20},{20... | collective-permute-start | bytes 3538952 | tf_op jit(solution)/shard_map/ppermute | solution.py:218
  168.8 76.3 %collective-permute-start.48 = (bf16[2,192,1536]{2,1,0:T(8,128)(2,1)}, bf16[2,192,1536]{2,1,0:T(8,128)(2,1)}, u32[]{:S(2)}, u32[]{:S(2)}) collective-permute-start(bf16[2,192,1536]{2,1,0:T(8,128)(2,1)} %fusion.13), channel_id=1, source_target_pairs={{0,8},{4,12},{8,0},{12,4},{1,9},{5,13},{9,1},{13,5},{2,10},{6,14},... | collective-permute-start | bytes 3538952 | tf_op jit(solution)/shard_map/ppermute | solution.py:209
  172.4 23.1 %collective-permute-start.24 = (bf16[256,768]{1,0:T(8,128)(2,1)S(1)}, bf16[256,768]{1,0:T(8,128)(2,1)S(1)}, u32[]{:S(2)}, u32[]{:S(2)}) collective-permute-start(bf16[256,768]{1,0:T(8,128)(2,1)S(1)} %get-tuple-element.132), channel_id=1, source_target_pairs={{0,2},{1,3},{2,0},{3,1},{4,6},{5,7},{6,4},{7,5},{8,10},{9,11},{10,... | collective-permute-start | bytes 1179656 | tf_op jit(solution)/shard_map/ppermute | solution.py:221
  177.1 18.4 %collective-permute-start.25 = (bf16[256,768]{1,0:T(8,128)(2,1)S(1)}, bf16[256,768]{1,0:T(8,128)(2,1)S(1)}, u32[]{:S(2)}, u32[]{:S(2)}) collective-permute-start(bf16[256,768]{1,0:T(8,128)(2,1)S(1)} %get-tuple-element.132), channel_id=1, source_target_pairs={{0,1},{1,0},{2,3},{3,2},{4,5},{5,4},{6,7},{7,6},{8,9},{9,8},{10,11... | collective-permute-start | bytes 1179656 | tf_op jit(solution)/shard_map/ppermute | solution.py:221
  183.9 25.9 %collective-permute-start.26 = (bf16[256,768]{1,0:T(8,128)(2,1)S(1)}, bf16[256,768]{1,0:T(8,128)(2,1)S(1)}, u32[]{:S(2)}, u32[]{:S(2)}) collective-permute-start(bf16[256,768]{1,0:T(8,128)(2,1)S(1)} %get-tuple-element.132), channel_id=1, source_target_pairs={{0,3},{1,2},{2,1},{3,0},{4,7},{5,6},{6,5},{7,4},{8,11},{9,10},{10,... | collective-permute-start | bytes 1179656 | tf_op jit(solution)/shard_map/ppermute | solution.py:221
  195.5 16.9 %collective-permute-start.29 = (bf16[256,768]{1,0:T(8,128)(2,1)S(1)}, bf16[256,768]{1,0:T(8,128)(2,1)}, u32[]{:S(2)}, u32[]{:S(2)}) collective-permute-start(bf16[256,768]{1,0:T(8,128)(2,1)S(1)} %get-tuple-element.85), channel_id=1, source_target_pairs={{0,4},{4,0},{8,12},{12,8},{1,5},{5,1},{9,13},{13,9},{2,6},{6,2},{1... | collective-permute-start | bytes 1179656 | tf_op jit(solution)/shard_map/ppermute | solution.py:206
  230.9 22.7 %collective-permute-start.30 = (bf16[512,768]{1,0:T(8,128)(2,1)}, bf16[512,768]{1,0:T(8,128)(2,1)}, u32[]{:S(2)}, u32[]{:S(2)}) collective-permute-start(bf16[512,768]{1,0:T(8,128)(2,1)} %pad_maximum_fusion.29), channel_id=1, source_target_pairs={{8,0},{12,4},{9,1},{13,5},{10,2},{14,6},{11,3},{15,7},{24,16},{28,... | collective-permute-start | bytes 2359304 | tf_op jit(solution)/shard_map/ppermute | solution.py:215
  241.6 32.5 %collective-permute-start.51 = (bf16[192,1536]{1,0:T(8,128)(2,1)}, bf16[192,1536]{1,0:T(8,128)(2,1)}, u32[]{:S(2)}, u32[]{:S(2)}) collective-permute-start(bf16[192,1536]{1,0:T(8,128)(2,1)} %fusion.21), channel_id=1, source_target_pairs={{0,8},{4,12},{8,0},{12,4},{1,9},{5,13},{9,1},{13,5},{2,10},{6,14},... | collective-permute-start | bytes 1769480 | tf_op jit(solution)/shard_map/ppermute | solution.py:209
  247.8 36.6 %collective-permute-start.49 = (bf16[192,1536]{1,0:T(8,128)(2,1)}, bf16[192,1536]{1,0:T(8,128)(2,1)}, u32[]{:S(2)}, u32[]{:S(2)}) collective-permute-start(bf16[192,1536]{1,0:T(8,128)(2,1)} %fusion.20), channel_id=1, source_target_pairs={{0,16},{16,0},{1,17},{17,1},{2,18},{18,2},{3,19},{19,3},{4,20},{20... | collective-permute-start | bytes 1769480 | tf_op jit(solution)/shard_map/ppermute | solution.py:218
  260.1 17.9 %collective-permute-start.31 = (bf16[256,768]{1,0:T(8,128)(2,1)}, bf16[256,768]{1,0:T(8,128)(2,1)}, u32[]{:S(2)}, u32[]{:S(2)}) collective-permute-start(bf16[256,768]{1,0:T(8,128)(2,1)} %slice.312), channel_id=1, source_target_pairs={{0,4},{4,0},{8,12},{12,8},{1,5},{5,1},{9,13},{13,9},{2,6},{6,2},{1... | collective-permute-start | bytes 1179656 | tf_op jit(solution)/shard_map/ppermute | solution.py:206
  267.8 40.6 %collective-permute-start.42 = (bf16[2,192,768]{2,1,0:T(8,128)(2,1)}, bf16[2,192,768]{2,1,0:T(8,128)(2,1)}, u32[]{:S(2)}, u32[]{:S(2)}) collective-permute-start(bf16[2,192,768]{2,1,0:T(8,128)(2,1)} %fusion.19), channel_id=1, source_target_pairs={{0,16},{16,0},{1,17},{17,1},{2,18},{18,2},{3,19},{19,3},{4,20},{20... | collective-permute-start | bytes 1769480 | tf_op jit(solution)/shard_map/ppermute | solution.py:218
  273.9 39.7 %collective-permute-start.40 = (bf16[2,192,768]{2,1,0:T(8,128)(2,1)}, bf16[2,192,768]{2,1,0:T(8,128)(2,1)}, u32[]{:S(2)}, u32[]{:S(2)}) collective-permute-start(bf16[2,192,768]{2,1,0:T(8,128)(2,1)} %fusion.18), channel_id=1, source_target_pairs={{0,8},{4,12},{8,0},{12,4},{1,9},{5,13},{9,1},{13,5},{2,10},{6,14},... | collective-permute-start | bytes 1769480 | tf_op jit(solution)/shard_map/ppermute | solution.py:209
  276.7 39.9 %collective-permute-start.54 = (bf16[192,1536]{1,0:T(8,128)(2,1)}, bf16[192,1536]{1,0:T(8,128)(2,1)}, u32[]{:S(2)}, u32[]{:S(2)}) collective-permute-start(bf16[192,1536]{1,0:T(8,128)(2,1)} %fusion.14), channel_id=1, source_target_pairs={{3,0},{2,1},{5,6},{4,7},{11,8},{10,9},{13,14},{12,15},{19,16},{18,... | collective-permute-start | bytes 1769480 | tf_op jit(solution)/shard_map/ppermute | solution.py:225
  278.0 69.6 %collective-permute-start.52 = (bf16[192,1536]{1,0:T(8,128)(2,1)}, bf16[192,1536]{1,0:T(8,128)(2,1)}, u32[]{:S(2)}, u32[]{:S(2)}) collective-permute-start(bf16[192,1536]{1,0:T(8,128)(2,1)} %fusion.14), channel_id=1, source_target_pairs={{1,0},{0,1},{7,6},{6,7},{9,8},{8,9},{15,14},{14,15},{17,16},{16,17... | collective-permute-start | bytes 1769480 | tf_op jit(solution)/shard_map/ppermute | solution.py:225
  304.9 41.8 %collective-permute-start.53 = (bf16[192,1536]{1,0:T(8,128)(2,1)}, bf16[192,1536]{1,0:T(8,128)(2,1)S(1)}, u32[]{:S(2)}, u32[]{:S(2)}) collective-permute-start(bf16[192,1536]{1,0:T(8,128)(2,1)} %fusion.17), channel_id=1, source_target_pairs={{2,0},{3,1},{4,6},{5,7},{10,8},{11,9},{12,14},{13,15},{18,16},{19,... | collective-permute-start | bytes 1769480 | tf_op jit(solution)/shard_map/ppermute | solution.py:225
  308.4 50.0 %collective-permute-start.32 = (bf16[256,768]{1,0:T(8,128)(2,1)S(1)}, bf16[256,768]{1,0:T(8,128)(2,1)S(1)}, u32[]{:S(2)}, u32[]{:S(2)}) collective-permute-start(bf16[256,768]{1,0:T(8,128)(2,1)S(1)} %subtract_convert_fusion), channel_id=1, source_target_pairs={{0,2},{1,3},{2,0},{3,1},{4,6},{5,7},{6,4},{7,5},{8,10},{9,11},{10,... | collective-permute-start | bytes 1179656 | tf_op jit(solution)/shard_map/ppermute | solution.py:221
  313.6 46.7 %collective-permute-start.33 = (bf16[256,768]{1,0:T(8,128)(2,1)S(1)}, bf16[256,768]{1,0:T(8,128)(2,1)S(1)}, u32[]{:S(2)}, u32[]{:S(2)}) collective-permute-start(bf16[256,768]{1,0:T(8,128)(2,1)S(1)} %subtract_convert_fusion), channel_id=1, source_target_pairs={{0,1},{1,0},{2,3},{3,2},{4,5},{5,4},{6,7},{7,6},{8,9},{9,8},{10,11... | collective-permute-start | bytes 1179656 | tf_op jit(solution)/shard_map/ppermute | solution.py:221
  316.6 45.0 %collective-permute-start.34 = (bf16[256,768]{1,0:T(8,128)(2,1)S(1)}, bf16[256,768]{1,0:T(8,128)(2,1)S(1)}, u32[]{:S(2)}, u32[]{:S(2)}) collective-permute-start(bf16[256,768]{1,0:T(8,128)(2,1)S(1)} %subtract_convert_fusion), channel_id=1, source_target_pairs={{0,3},{1,2},{2,1},{3,0},{4,7},{5,6},{6,5},{7,4},{8,11},{9,10},{10,... | collective-permute-start | bytes 1179656 | tf_op jit(solution)/shard_map/ppermute | solution.py:221
  346.7 6.7 %collective-permute-start.43 = (bf16[192,768]{1,0:T(8,128)(2,1)S(1)}, bf16[192,768]{1,0:T(8,128)(2,1)S(1)}, u32[]{:S(2)}, u32[]{:S(2)}) collective-permute-start(bf16[192,768]{1,0:T(8,128)(2,1)S(1)} %fusion.30), channel_id=1, source_target_pairs={{0,8},{4,12},{8,0},{12,4},{1,9},{5,13},{9,1},{13,5},{2,10},{6,14},... | collective-permute-start | bytes 884744 | tf_op jit(solution)/shard_map/ppermute | solution.py:209
  347.6 8.7 %collective-permute-start.41 = (bf16[192,768]{1,0:T(8,128)(2,1)S(1)}, bf16[192,768]{1,0:T(8,128)(2,1)S(1)}, u32[]{:S(2)}, u32[]{:S(2)}) collective-permute-start(bf16[192,768]{1,0:T(8,128)(2,1)S(1)} %fusion.29), channel_id=1, source_target_pairs={{0,16},{16,0},{1,17},{17,1},{2,18},{18,2},{3,19},{19,3},{4,20},{20... | collective-permute-start | bytes 884744 | tf_op jit(solution)/shard_map/ppermute | solution.py:218
  353.5 24.2 %collective-permute-start.55 = (f32[96,1536]{1,0:T(8,128)}, f32[96,1536]{1,0:T(8,128)}, u32[]{:S(2)}, u32[]{:S(2)}) collective-permute-start(f32[96,1536]{1,0:T(8,128)} %dynamic-slice_bitcast_fusion), channel_id=1, source_target_pairs={{0,4},{1,5},{6,2},{7,3},{8,12},{9,13},{14,10},{15,11},{16,20},{17,... | collective-permute-start | bytes 1769480 | tf_op jit(solution)/shard_map/ppermute | solution.py:225
  356.3 13.5 %collective-permute-start.46 = (bf16[192,768]{1,0:T(8,128)(2,1)}, bf16[192,768]{1,0:T(8,128)(2,1)}, u32[]{:S(2)}, u32[]{:S(2)}) collective-permute-start(bf16[192,768]{1,0:T(8,128)(2,1)} %fusion.22), channel_id=1, source_target_pairs={{3,0},{2,1},{5,6},{4,7},{11,8},{10,9},{13,14},{12,15},{19,16},{18,... | collective-permute-start | bytes 884744 | tf_op jit(solution)/shard_map/ppermute | solution.py:225
  358.4 16.6 %collective-permute-start.44 = (bf16[192,768]{1,0:T(8,128)(2,1)}, bf16[192,768]{1,0:T(8,128)(2,1)}, u32[]{:S(2)}, u32[]{:S(2)}) collective-permute-start(bf16[192,768]{1,0:T(8,128)(2,1)} %fusion.22), channel_id=1, source_target_pairs={{1,0},{0,1},{7,6},{6,7},{9,8},{8,9},{15,14},{14,15},{17,16},{16,17... | collective-permute-start | bytes 884744 | tf_op jit(solution)/shard_map/ppermute | solution.py:225
  360.3 14.6 %collective-permute-start.45 = (bf16[192,768]{1,0:T(8,128)(2,1)}, bf16[192,768]{1,0:T(8,128)(2,1)}, u32[]{:S(2)}, u32[]{:S(2)}) collective-permute-start(bf16[192,768]{1,0:T(8,128)(2,1)} %fusion.28), channel_id=1, source_target_pairs={{2,0},{3,1},{4,6},{5,7},{10,8},{11,9},{12,14},{13,15},{18,16},{19,... | collective-permute-start | bytes 884744 | tf_op jit(solution)/shard_map/ppermute | solution.py:225
  (76 other events, 468.3 us)

commit v2 on v1

--- a/solution.py
+++ b/solution.py
@@ -189,16 +189,19 @@
     )(meta, queries, near_kv, near_kv, far_kv, far_kv, grads, logs)
 
 
+def after(value, *gates):
+    return lax.optimization_barrier((value, *gates))[0]
+
+
 class Place:
     def __init__(self):
         self.n_shard = lax.axis_size("shard")
         self.n_ctx = lax.axis_size("ctx")
         self.n_tp = lax.axis_size("tp")
         self.shard = lax.axis_index("shard")
-        ctx = lax.axis_index("ctx")
-        self.ctx = ctx
-        self.half = ctx // 2
-        self.core = ctx % 2
+        self.ctx = lax.axis_index("ctx")
+        self.half = self.ctx // 2
+        self.core = self.ctx % 2
         self.tp = lax.axis_index("tp")
         self.home = self.core == self.tp // 2
 
@@ -220,100 +223,63 @@
     def tp_swap(self, value, mask):
         return lax.ppermute(value, "tp", [(i, i ^ mask) for i in range(self.n_tp)])
 
-    def mixed(self, value, pairs):
-        flat = [(a * self.n_tp + b, c * self.n_tp + d) for (a, b), (c, d) in pairs]
-        return lax.ppermute(value, ("ctx", "tp"), flat)
-
-    def to_home(self, value):
-        return self.mixed(
-            value,
-            [((2 * h + 1 - z // 2, z), (2 * h + z // 2, z)) for h in (0, 1) for z in range(4)],
-        )
-
-    def from_home(self, value):
-        return self.mixed(
-            value,
-            [((2 * h + z // 2, z), (2 * h + 1 - z // 2, z)) for h in (0, 1) for z in range(4)],
-        )
-
-    def spread(self, value, mask):
-        return self.mixed(
-            value,
-            [((2 * h + z // 2, z), (2 * h + z // 2, z ^ mask)) for h in (0, 1) for z in range(4)],
-        )
-
-    def collect(self, value, mask):
-        return self.mixed(
-            value,
-            [((2 * h + z // 2, z ^ mask), (2 * h + z // 2, z)) for h in (0, 1) for z in range(4)],
-        )
-
-    def ordered(self, flag, mine, other):
+    def ordered(self, flag, mine, other, axis=0):
         first = jnp.where(flag == 0, mine, other)
         second = jnp.where(flag == 0, other, mine)
-        return jnp.stack([first, second], 0)
+        return jnp.stack([first, second], axis)
+
+
+    def own_block(self, piece, far):
+        kept = jnp.where(self.home, piece, far)
+        sent = jnp.where(self.home, far, piece)
+        return self.ordered(self.core, kept, self.core_swap(sent)).reshape(-1, piece.shape[1])
 
     def over_shards(self, value):
         if self.n_shard == 2:
             return self.ordered(self.shard, value, self.shard_swap(value))
         return lax.all_gather(value, "shard", axis=0)
 
-    def over_halves(self, value):
-        return self.ordered(self.half, value, self.half_swap(value))
-
-    def gather(self, piece):
-        part, width = piece.shape
-        both = self.ordered(self.core, piece, self.to_home(piece)).reshape(2 * part, width)
-        near, far, cross = (self.spread(both, mask) for mask in (1, 2, 3))
-        first = jnp.where(self.home, both, far)
-        second = jnp.where(self.home, near, cross)
-        first = self.over_halves(self.over_shards(first))
-        first = jnp.moveaxis(first, 0, 1).reshape(-1, width)
-        second = self.over_shards(self.over_halves(second)).reshape(-1, width)
-        return first, second
-
-    def reduce_halves(self, value, axis):
+    def rows_half_first(self, block):
+        value = self.over_shards(self.ordered(self.half, block, self.half_swap(block)))
+        return value.reshape(-1, block.shape[1])
+
+    def rows_shard_first(self, block):
+        value = self.over_shards(block)
+        value = self.ordered(self.half, value, self.half_swap(value), 1)
+        return value.reshape(-1, block.shape[1])
+
+
+    def split_rows(self, value):
+        rows, width = value.shape
+        return value.reshape(self.n_shard, 2, rows // (2 * self.n_shard), width)
+
+    def half_step(self, value, axis):
         sent = lax.dynamic_index_in_dim(value, 1 - self.half, axis, False).astype(LOW)
         kept = lax.dynamic_index_in_dim(value, self.half, axis, False)
-        return kept + self.half_swap(sent).astype(SINGLE)
-
-    def reduce_shards(self, value):
+        return kept, self.half_swap(sent)
+
+    def shard_step(self, value):
         if self.n_shard == 2:
             sent = lax.dynamic_index_in_dim(value, 1 - self.shard, 0, False).astype(LOW)
             kept = lax.dynamic_index_in_dim(value, self.shard, 0, False)
-            return kept + self.shard_swap(sent).astype(SINGLE)
-        return lax.psum_scatter(value, "shard", scatter_dimension=0, tiled=False)
-
-    def scatter(self, first, second):
-        rows, width = first.shape
-        shape = (self.n_shard, 2, rows // (2 * self.n_shard), width)
-        first = self.reduce_shards(self.reduce_halves(first.reshape(shape), 1))
-        second = self.reduce_halves(self.reduce_shards(second.reshape(shape)), 0)
-        low_first, low_second = first.astype(LOW), second.astype(LOW)
-        near = self.collect(low_second, 1)
-        far = self.mixed_far(low_first)
-        cross = self.mixed_cross(low_second)
-        total = first + near.astype(SINGLE) + far.astype(SINGLE) + cross.astype(SINGLE)
-        pieces = total.reshape(2, -1, width)
-        sent = lax.dynamic_index_in_dim(pieces, 1 - self.core, 0, False)
+            return kept, self.shard_swap(sent)
+        kept = lax.psum_scatter(value, "shard", scatter_dimension=0, tiled=False)
+        return kept, jnp.zeros_like(kept, LOW)
+
+    def block_step(self, value):
+        pieces = value.reshape(2, -1, value.shape[1])
+        sent = lax.dynamic_index_in_dim(pieces, 1 - self.core, 0, False).astype(LOW)
         kept = lax.dynamic_index_in_dim(pieces, self.core, 0, False)
-        return jnp.where(self.home, kept, self.from_home(sent))
-
-    def mixed_far(self, value):
-        return self.collect(value, 2)
-
-    def mixed_cross(self, value):
-        return self.collect(value, 3)
-
-    def over_tp(self, value):
-        got = [value] + [self.tp_swap(value, mask) for mask in (1, 2, 3)]
-        slots = []
-        for slot in range(4):
-            item = got[3]
-            for mask in (0, 1, 2):
-                item = jnp.where((self.tp ^ slot) == mask, got[mask], item)
-            slots.append(item)
-        return jnp.stack(slots, 0)
+        got = self.core_swap(sent).astype(SINGLE)
+        sent = jnp.where(self.home, got, kept).astype(LOW)
+        return jnp.where(self.home, kept, got), self.tp_swap(sent, 2)
+
+    def tp_far(self, value):
+        return self.ordered(self.tp // 2, value, self.tp_swap(value, 2))
+
+    def tp_all(self, pair):
+        value = self.ordered(self.tp % 2, pair, self.tp_swap(pair, 1), 1)
+        return value.reshape(4, *pair.shape[1:])
 
     def total(self, value):
         value = value + self.core_swap(value)
@@ -325,8 +291,16 @@
         return value + self.tp_swap(value, 2)
 
 
-def columns(first, second, start, size):
-    return jnp.concatenate([first[:, start : start + size], second[:, start : start + size]], 1)
+def added(step, *gates):
+    kept, arriving = step
+    return kept + after(arriving, *gates).astype(SINGLE)
+
+
+def interleaved(first, second, width):
+    parts = []
+    for start in range(0, first.shape[1], width):
+        parts += [first[:, start : start + width], second[:, start : start + width]]
+    return jnp.concatenate(parts, 1)
 
 
 def shards(
@@ -350,51 +324,61 @@
     head_width = entry_weight.shape[2]
     units = hidden_weight.shape[1]
 
-    entry_piece = jnp.moveaxis(entry_weight, 0, 1).reshape(part, 3 * head_width)
-    rest_piece = jnp.concatenate([exit_weight.T, hidden_weight, return_weight.T], 1)
-    entry_first, entry_second = place.gather(entry_piece)
-    rest_first, rest_second = place.gather(rest_piece)
-    weight_q = columns(entry_first, entry_second, 0, head_width)
-    weight_kv = jnp.concatenate(
-        [columns(entry_first, entry_second, at * head_width, head_width) for at in (1, 2)], 1
-    )
-    exit_t = columns(rest_first, rest_second, 0, head_width)
-    hidden_full = columns(rest_first, rest_second, head_width, units)
-    return_t = columns(rest_first, rest_second, head_width + units, units)
+    width = 2 * head_width
+
+    piece_a = jnp.concatenate([entry_weight[1], entry_weight[2], entry_weight[0], exit_weight.T], 1)
+    piece_b = jnp.concatenate([hidden_weight, return_weight.T], 1)
     biases = jnp.concatenate([entry_bias.reshape(-1), hidden_bias])
-    bias_got = [biases] + [place.tp_swap(biases, mask) for mask in (1, 2, 3)]
-    bias_first = jnp.where(place.home, bias_got[0], bias_got[2])
-    bias_second = jnp.where(place.home, bias_got[1], bias_got[3])
-    bias_two = jnp.stack([bias_first, bias_second])
+    far_a = place.tp_swap(piece_a, 2)
+    bias_mine = jnp.where(place.home, biases, place.tp_swap(biases, 2))
+    bias_two = jnp.stack([bias_mine, place.tp_swap(bias_mine, 1)])
     bias_q = bias_two[:, :head_width].reshape(-1)
-    bias_v = bias_two[:, head_width : 2 * head_width].reshape(-1)
-    bias_h = bias_two[:, 2 * head_width :].reshape(-1)
+    bias_v = bias_two[:, head_width:width].reshape(-1)
+    bias_h = bias_two[:, width:].reshape(-1)
+    mine_a = place.own_block(piece_a, far_a)
+    other_a = place.tp_swap(mine_a, 1)
+    block_kv = interleaved(mine_a[:, :width], other_a[:, :width], head_width)
+    block_qe = interleaved(mine_a[:, width:], other_a[:, width:], head_width)
+    weight_kv = place.rows_half_first(block_kv)
+    weight_qe = place.rows_shard_first(block_qe)
+    weight_q, exit_t = weight_qe[:, :width], weight_qe[:, width:]
+    piece_b = after(piece_b, other_a)
+    mine_b = place.own_block(piece_b, place.tp_swap(piece_b, 2))
+    other_b = place.tp_swap(mine_b, 1)
 
     length = lax.dynamic_index_in_dim(lengths, place.tp, 0, False)
-    stream_part = lax.dynamic_index_in_dim(tokens, place.tp, 0, False).astype(SINGLE)
+    tokens_low, cot_low = (
+        lax.dynamic_index_in_dim(item, place.tp, 0, False) for item in (tokens, cotangent)
+    )
+    stream_part = after(tokens_low, far_a).astype(SINGLE)
     stream = jnp.concatenate([stream_part, -jnp.sum(stream_part, -1, keepdims=True)], 1)
     first_inverse = lax.rsqrt(row_mean(stream * stream) + EPSILON)
     first_unit = stream * first_inverse
     normed_own = (first_unit * first_gain).astype(LOW)
-    first_normed = jnp.concatenate([normed_own, place.core_swap(normed_own)], 0)
-
     position = place.ctx * local + jnp.arange(local, dtype=jnp.int32)
     valid = (position < length).astype(SINGLE)[:, None]
-    cot_rows = lax.dynamic_index_in_dim(cotangent, place.tp, 0, False).astype(SINGLE) * valid
+    cot_rows = cot_low.astype(SINGLE) * valid
     cot_full = jnp.concatenate([cot_rows, jnp.zeros((local, 1), SINGLE)], 1)
-    returned_grad_own = (cot_full - row_mean(cot_full)).astype(LOW)
-    returned_grad = jnp.concatenate([returned_grad_own, place.core_swap(returned_grad_own)], 0)
-    return_bias_grad = jnp.sum(returned_grad_own.astype(SINGLE), 0)
+    returned_own = (cot_full - row_mean(cot_full)).astype(LOW)
+    own_two = jnp.concatenate([normed_own, returned_own], 1)
+    all_two = jnp.concatenate([own_two, place.core_swap(own_two)], 0)
+    wide = narrow + 1
+    first_normed, returned_grad = all_two[:, :wide], all_two[:, wide:]
 
     bias_kv = jnp.concatenate([jnp.zeros_like(bias_v), bias_v])
     near_kv = (dot(first_normed, weight_kv) + bias_kv).astype(LOW)
     far_kv = place.half_up(near_kv)
+    block_h = jnp.concatenate([mine_b[:, :units], other_b[:, :units]], 1)
+    block_r = jnp.concatenate([mine_b[:, units:], other_b[:, units:]], 1)
+    block_h, block_r = after((block_h, block_r), near_kv, weight_qe)
+    hidden_full = place.rows_half_first(block_h)
+    return_t = place.rows_shard_first(block_r)
     queries = (dot(first_normed, weight_q) + bias_q).astype(LOW)
     meta = jnp.stack([place.half, place.core, length]).astype(jnp.int32)
     attended, logs = attention_forward(meta, queries, near_kv, far_kv)
 
-    def joined(partial):
-        return partial[:local] + place.core_swap(partial[local:].astype(LOW)).astype(SINGLE)
+    def joined(partial, *gates):
+        return added((partial[:local], place.core_swap(partial[local:].astype(LOW))), *gates)
 
     branch = joined(dot_nt(attended, exit_t)) + exit_bias
     middle = stream + branch - row_mean(branch)
@@ -408,10 +392,17 @@
     )
     activated_low = activated.astype(LOW)
     hidden_grad = gelu_pull(dot(returned_grad, return_t))[0].astype(LOW)
-    second_grad = joined(dot_nt(hidden_grad, hidden_full))
-    returned = joined(dot_nt(activated_low, return_t)) + return_bias
+    second_part = dot_nt(hidden_grad, hidden_full)
+    returned_part = dot_nt(activated_low, return_t)
+    second_grad = joined(second_part)
+    returned = joined(returned_part, second_part) + return_bias
     full_stream = middle + returned - row_mean(returned)
-    result = place.over_tp(full_stream.astype(LOW))[:, :, :narrow]
+    result_own = full_stream.astype(LOW)
+
+    hidden_weight_grad = dot_tn(second_normed, hidden_grad)
+    return_weight_grad = dot_tn(returned_grad, after(activated_low, second_part))
+    step_h = place.half_step(place.split_rows(hidden_weight_grad), 1)
+    step_r = place.shard_step(place.split_rows(return_weight_grad))
 
     second_gain_grad = jnp.sum(second_grad * second_unit, 0)
     second_scaled = second_grad * second_gain
@@ -419,56 +410,67 @@
         second_scaled - second_unit * row_mean(second_scaled * second_unit)
     )
     branch_own = (middle_grad - row_mean(middle_grad)).astype(LOW)
-    exit_bias_grad = jnp.sum(branch_own.astype(SINGLE), 0)
     branch_grad = jnp.concatenate([branch_own, place.core_swap(branch_own)], 0)
+    result_far = place.tp_far(result_own)
     attended_grad = dot(branch_grad, exit_t).astype(LOW)
     query_low, near_k, near_v, far_k, far_v = attention_backward(
         meta, queries, near_kv, far_kv, attended_grad, logs
     )
     back_kv = place.half_down(jnp.concatenate([far_k, far_v], 1))
-    kv_low = (jnp.concatenate([near_k, near_v], 1) + back_kv.astype(SINGLE)).astype(LOW)
-    first_grad = joined(dot_nt(query_low, weight_q) + dot_nt(kv_low, weight_kv))
-    first_gain_grad = jnp.sum(first_grad * first_unit, 0)
+    result_all = place.tp_all(after(result_far, query_low))
+    step_h = place.shard_step(added(step_h, query_low))
+    step_r = place.half_step(added(step_r, query_low), 0)
+    query_weight_grad = dot_tn(first_normed, query_low)
+    exit_weight_grad = dot_tn(branch_grad, attended)
+    query_part = dot_nt(query_low, weight_q)
+    kv_low = (
+        jnp.concatenate([near_k, near_v], 1)
+        + after(back_kv, query_weight_grad, exit_weight_grad, query_part).astype(SINGLE)
+    ).astype(LOW)
+    first_part = query_part + dot_nt(kv_low, weight_kv)
+    first_grad = joined(first_part)
     first_scaled = first_grad * first_gain
     stream_grad = middle_grad + first_inverse * (
         first_scaled - first_unit * row_mean(first_scaled * first_unit)
     )
     tokens_rows = (stream_grad - stream_grad[:, narrow:]).astype(LOW)
-    tokens_grad = place.over_tp(tokens_rows)[:, :, :narrow]
-
-    hidden_weight_grad = dot_tn(second_normed, hidden_grad)
-    return_weight_grad = dot_tn(returned_grad, activated_low)
-    mlp = place.scatter(
-        *(
-            jnp.concatenate(
-                [hidden_weight_grad[:, cut], return_weight_grad[:, cut]], 1
-            )
-            for cut in (slice(0, units), slice(units, None))
-        )
-    )
-    query_weight_grad = dot_tn(first_normed, query_low)
+    tokens_far = place.tp_far(tokens_rows)
+
+    sum_h, sum_r = added(step_h, first_part), added(step_r, first_part)
+    mlp = (
+        jnp.concatenate([sum_h[:, :units], sum_r[:, :units]], 1),
+        place.tp_swap(
+            jnp.concatenate([sum_h[:, units:], sum_r[:, units:]], 1).astype(LOW), 1
+        ),
+    )
     kv_weight_grad = dot_tn(first_normed, kv_low)
-    exit_weight_grad = dot_tn(branch_grad, attended)
-    width = 2 * head_width
-    heads = place.scatter(
-        *(
-            jnp.concatenate(
-                [
-                    query_weight_grad[:, at : at + head_width],
-                    kv_weight_grad[:, at : at + head_width],
-                    kv_weight_grad[:, width + at : width + at + head_width],
-                    exit_weight_grad[:, at : at + head_width],
-                ],
-                1,
-            )
-            for at in (0, head_width)
-        )
-    )
-    entry_grad = jnp.moveaxis(heads[:, : 3 * head_width].reshape(part, 3, head_width), 1, 0)
-    exit_grad = heads[:, 3 * head_width :].T
+    step_kv = place.half_step(place.split_rows(kv_weight_grad), 1)
+    step_qe = place.shard_step(
+        place.split_rows(jnp.concatenate([query_weight_grad, exit_weight_grad], 1))
+    )
+    mlp = place.block_step(added(mlp, tokens_rows))
+    step_kv = place.shard_step(added(step_kv, tokens_rows))
+    step_qe = place.half_step(added(step_qe, tokens_rows), 0)
+    tokens_all = place.tp_all(tokens_far)
+    sums = jnp.concatenate([added(step_qe), added(step_kv)], 1)
+    sums = [
+        jnp.concatenate([sums[:, at * width + low : at * width + low + head_width] for at in range(4)], 1)
+        for low in (0, head_width)
+    ]
+    heads = place.block_step(added((sums[0], place.tp_swap(sums[1].astype(LOW), 1))))
+    mlp = added(mlp, tokens_all)
+    heads = added(heads, tokens_all)
+    result = after(result_all, tokens_rows)[:, :, :narrow]
+    tokens_grad = tokens_all[:, :, :narrow]
+    at = lambda index: heads[:, index * head_width : (index + 1) * head_width]
+    entry_grad = jnp.stack([at(0), at(2), at(3)])
+    exit_grad = at(1).T
     hidden_out = mlp[:, :units]
     return_out = mlp[:, units:].T
 
+    return_bias_grad = jnp.sum(returned_own.astype(SINGLE), 0)
+    exit_bias_grad = jnp.sum(branch_own.astype(SINGLE), 0)
+    first_gain_grad = jnp.sum(first_grad * first_unit, 0)
     query_sum = jnp.sum(query_low.astype(SINGLE), 0).reshape(2, head_width)
     value_sum = jnp.sum(kv_low[:, width:].astype(SINGLE), 0).reshape(2, head_width)
     hidden_sum = jnp.sum(hidden_grad.astype(SINGLE), 0).reshape(2, units)
@@ -484,19 +486,18 @@
         [first_gain_grad, exit_bias_grad, second_gain_grad, return_bias_grad] + slots
     )
     vectors = place.total(vectors)
-    wide = narrow + 1
-    mine = lax.dynamic_index_in_dim(vectors[4 * wide :].reshape(4, -1), place.tp, 0, False)
+    own = lax.dynamic_index_in_dim(vectors[4 * wide :].reshape(4, -1), place.tp, 0, False)
     return (
         result,
         tokens_grad,
         vectors[:wide],
         entry_grad,
-        mine[:width].reshape(2, head_width),
+        own[:width].reshape(2, head_width),
         exit_grad,
         vectors[wide : 2 * wide],
         vectors[2 * wide : 3 * wide],
         hidden_out,
-        mine[width:],
+        own[width:],
         return_out,
         vectors[3 * wide : 4 * wide],
     )

time: 389 us -> 334 us (0.86)
  starting transfers between devices: 96.1 us -> 56.3 us
  matrix products: 31.8 us -> 24.6 us
  local copies, waits for them, and re-layouts: 52.3 us -> 48.4 us
    ppermute x11 -> x16, waiting for transfers between devices: 29.3 us -> 71.5 us  [tp_swap(): return lax.ppermute(value, 'tp', [(i, i ^ mask) for i in range(self.n_tp)])]
    ppermute x16 -> x0, waiting for transfers between devices: 41.2 us -> none  [mixed(): return lax.ppermute(value, ('ctx', 'tp'), flat)]
    ppermute x16 -> x0, starting transfers between devices: 35.3 us -> none  [mixed(): return lax.ppermute(value, ('ctx', 'tp'), flat)]
    ppermute x9, waiting for transfers between devices: 5.54 us -> 37.8 us  [shard_swap(): return lax.ppermute(value, 'shard', [(0, 1), (1, 0)])]
    ppermute x9, waiting for transfers between devices: 36.5 us -> 7.22 us  [half_swap(): return lax.ppermute(value, 'ctx', [(i, i ^ 2) for i in range(self.n_ctx)])]
    slice x13 -> x16, local copies, waits for them, and re-layouts: 10.6 us -> 1.41 us  [the longest x1 0.68 us: shards(): own[width:]]
    dot_general x5, matrix products: 14.8 us -> 9.15 us  [dot(): return jnp.dot(left, right, preferred_element_type=SINGLE)]
    ppermute x1, waiting for transfers between devices: 5.33 us -> 0.01 us  [half_down(): return lax.ppermute(value, 'ctx', [(2, 0), (3, 1)])]
  transfers between devices with their start and end apart: 56 -> 48, of which waited for: 21 -> 18; matrix products, arithmetic and copies ran while one was open for 29% -> 27% of each run, Pallas kernels for 6% -> 7%
where the time goes in v2:
time: 334 us; the launch traced here: 327 us
  waiting for transfers between devices  131 us (39%)
  starting transfers between devices  56.3 us (17%)
  local copies, waits for them, and re-layouts  48.4 us (14%)
  other arithmetic  40.7 us (12%)
  matrix products  24.6 us (7%)
  Pallas kernels  23.9 us (7%)
    ppermute x16, waiting for transfers between devices, tp_swap(): return lax.ppermute(value, 'tp', [(i, i ^ mask) for i in range(self.n_tp)])  71.5 us
    ppermute x9, waiting for transfers between devices, shard_swap(): return lax.ppermute(value, 'shard', [(0, 1), (1, 0)])  37.8 us
    ppermute x16, starting transfers between devices, tp_swap(): return lax.ppermute(value, 'tp', [(i, i ^ mask) for i in range(self.n_tp)])  23.9 us
    unnamed x131, local copies, waits for them, and re-layouts  17 us
    ppermute x9, starting transfers between devices, half_swap(): return lax.ppermute(value, 'ctx', [(i, i ^ 2) for i in range(self.n_ctx)])  15.5 us
    pallas_call x1, Pallas kernels, attention_backward(): pl.pallas_call(backward_kernel, grid_spec=pltpu.PrefetchScalarGridSpec(nu...  13.4 us
    add x10, other arithmetic, added(): return kept + after(arriving, *gates).astype(SINGLE)  13.2 us
    ppermute x1, waiting for transfers between devices, half_up(): return lax.ppermute(value, 'ctx', [(0, 2), (1, 3)])  12.4 us
  transfers between devices with their start and end apart: 48, of which 18 were waited for; matrix products, arithmetic and copies ran while one was open for 27% of the time, Pallas kernels for 7%

profile of v2, /device:TPU:0, one launch (start us, length us, event | category | flops | bytes accessed | tf_op | source)
XLA Modules:
  0.0 327.2 jit_solution(6841079479093090729)
XLA Ops:
  2.1 4.1 %collective-permute-start.6 = (f32[1152]{0:T(1024)S(1)}, f32[1152]{0:T(1024)S(1)}, u32[]{:S(2)}, u32[]{:S(2)}) collective-permute-start(f32[1152]{0:T(1024)S(1)} %constant_dynamic-update-slice_fusion.9), channel_id=1, source_target_pairs={{0,2},{1,3},{2,0},{3,1},{4,6},{5,7},{6,4},{7,5},{8,10},{9,11},{10,... | collective-permute-start | bytes 13832 | tf_op jit(solution)/shard_map/ppermute | solution.py:224
  9.4 3.5 %constant_dynamic-slice_fusion.1 = (bf16[1,256,767]{1,0,2:T(2,128)(2,1)S(1)}, bf16[1,256,767]{1,0,2:T(2,128)(2,1)S(1)}) fusion(bf16[4,256,767]{1,0,2:T(4,128)(2,1)} %param.25, s32[]{:T(128)S(6)} %select_n.328, bf16[4,256,767]{1,0,2:T(4,128)(2,1)} %param.13), kind=kLoop, calls=%fused_computation.194 | loop fusion | bytes 1570820 | tf_op jit(solution)/shard_map/jit(dynamic_index_in_dim)/dynamic_slice | solution.py:351
  15.8 1.9 collective-permute-start.7
  24.0 7.5 %collective-permute-done.3 = bf16[192,768]{1,0:T(8,128)(2,1)S(1)} collective-permute-done((bf16[192,768]{1,0:T(8,128)(2,1)S(1)}, bf16[192,768]{1,0:T(8,128)(2,1)S(1)}, u32[]{:S(2)}, u32[]{:S(2)}) %collective-permute-start.3) | collective-permute-done | bytes 294944 | tf_op jit(solution)/shard_map/ppermute | solution.py:224
  31.5 2.6 collective-permute-start.13
  37.6 9.3 %collective-permute-done.13 = bf16[96,1536]{1,0:T(8,128)(2,1)S(1)} collective-permute-done((bf16[96,1536]{1,0:T(8,128)(2,1)S(1)}, bf16[96,1536]{1,0:T(8,128)(2,1)S(1)}, u32[]{:S(2)}, u32[]{:S(2)}) %collective-permute-start.13) | collective-permute-done | bytes 294944 | tf_op jit(solution)/shard_map/ppermute | solution.py:224
  47.3 1.6 collective-permute-start.5
  51.6 13.1 %collective-permute-done.9 = bf16[2,192,768]{2,1,0:T(8,128)(2,1)S(1)} collective-permute-done((bf16[2,192,768]{2,1,0:T(8,128)(2,1)S(1)}, bf16[2,192,768]{2,1,0:T(8,128)(2,1)S(1)}, u32[]{:S(2)}, u32[]{:S(2)}) %collective-permute-start.9) | collective-permute-done | bytes 589856 | tf_op jit(solution)/shard_map/ppermute | solution.py:221
  65.9 3.4 %collective-permute-start.10 = (bf16[512,768]{1,0:T(8,128)(2,1)S(1)}, bf16[512,768]{1,0:T(8,128)(2,1)}, u32[]{:S(2)}, u32[]{:S(2)}) collective-permute-start(bf16[512,768]{1,0:T(8,128)(2,1)S(1)} %add_convert_fusion.k_ref.v_ref), channel_id=1, source_target_pairs={{0,8},{4,12},{1,9},{5,13},{2,10},{6,14},{3,11},{7,15},{16,24},{20,... | collective-permute-start | bytes 2359304 | tf_op jit(solution)/shard_map/ppermute | solution.py:215
  73.7 12.4 %collective-permute-done.10.kf_ref.vf_ref = bf16[512,768]{1,0:T(8,128)(2,1)} collective-permute-done((bf16[512,768]{1,0:T(8,128)(2,1)S(1)}, bf16[512,768]{1,0:T(8,128)(2,1)}, u32[]{:S(2)}, u32[]{:S(2)}) %collective-permute-start.10) | collective-permute-done | bytes 786464 | tf_op jit(solution)/shard_map/ppermute | solution.py:215
  86.2 10.5 %attend.1 = (bf16[512,384]{1,0:T(8,128)(2,1)}, f32[3,2,512]{2,1,0:T(2,128)}) custom-call(s32[3]{0:T(128)} %pad_add_fusion.meta, bf16[512,384]{1,0:T(8,128)(2,1)} %fusion.8.q_ref, bf16[512,768]{1,0:T(8,128)(2,1)} %copy-done.58, bf16[512,768]{1,0:T(8,128)(2,1)} %copy-done.58, bf16[512,768]{1,0:T(8,128)(2,1)} %collective-permute-done.10.kf_ref.vf_ref, ...), custom_call_target="tpu_custom_call" | custom-call | flops 1610612736 | bytes 2752512 | tf_op jit(solution)/shard_map/attend/pallas_call | solution.py:85
  96.7 1.6 fusion.26
  102.7 2.7 collective-permute-start.19
  106.5 21.8 %collective-permute-done.17 = bf16[2,192,1536]{2,1,0:T(8,128)(2,1)S(1)} collective-permute-done((bf16[2,192,1536]{2,1,0:T(8,128)(2,1)S(1)}, bf16[2,192,1536]{2,1,0:T(8,128)(2,1)S(1)}, u32[]{:S(2)}, u32[]{:S(2)}) %collective-permute-start.17) | collective-permute-done | bytes 1179680 | tf_op jit(solution)/shard_map/ppermute | solution.py:221
  128.5 3.3 collective-permute-done.19
  132.4 2.0 multiply_convert_fusion
  134.4 3.7 %convert_reduce_fusion = (f32[1536]{0:T(1024)}, bf16[512,1536]{1,0:T(8,128)(2,1)S(1)}) fusion(f32[512,1536]{1,0:T(8,128)S(1)} %get-tuple-element.171, bf16[768,1536]{1,0:T(8,128)(2,1)S(1)} %bitcast.190, bf16[512,1536]{1,0:T(8,128)(2,1)S(1)} %copy-done.3), kind=kOutput, calls=%fused_computation.10 | convolution fusion | flops 1225259520 | bytes 7870464 | tf_op jit(solution)/shard_map/dot_general | solution.py:24
  138.1 2.6 fusion.72
  146.6 3.1 fusion.13
  150.9 1.6 copy-done.1
  154.4 2.2 copy-done
  157.8 1.7 collective-permute-start.41
  162.0 19.4 %collective-permute-done.21 = bf16[256,768]{1,0:T(8,128)(2,1)S(1)} collective-permute-done((bf16[256,768]{1,0:T(8,128)(2,1)S(1)}, bf16[256,768]{1,0:T(8,128)(2,1)S(1)}, u32[]{:S(2)}, u32[]{:S(2)}) %collective-permute-start.21) | collective-permute-done | bytes 393248 | tf_op jit(solution)/shard_map/ppermute | solution.py:224
  183.7 13.4 %attend_back.1 = (bf16[512,384]{1,0:T(8,128)(2,1)}, f32[512,384]{1,0:T(8,128)}, f32[512,384]{1,0:T(8,128)}, bf16[512,384]{1,0:T(8,128)(2,1)}, bf16[512,384]{1,0:T(8,128)(2,1)}) custom-call(s32[3]{0:T(128)} %pad_add_fusion.meta, bf16[512,384]{1,0:T(8,128)(2,1)} %fusion.8.q_ref, bf16[512,768]{1,0:T(8,128)(2,1)} %copy-done.58, bf16[512,768]{1,0:T(8,128)(2,1)} %copy-done.58, ...), custom_call_target="tpu_custom_call" | custom-call | flops 4026531840 | bytes 5898240 | tf_op jit(solution)/shard_map/attend_back/pallas_call | solution.py:160
  197.1 2.2 pad_maximum_fusion.15
  205.0 3.3 %copy.41 = f32[768,768]{1,0:T(8,128)} copy(f32[768,768]{0,1:T(8,128)} %pad_maximum_fusion.2) | data formatting | bytes 4718592 | tf_op jit(solution)/shard_map/concatenate | solution.py:449
  208.4 2.3 fusion.21
  212.5 2.3 bitcast_add_fusion
  215.8 3.5 %collective-permute-start.44 = (bf16[192,1536]{1,0:T(8,128)(2,1)}, bf16[192,1536]{1,0:T(8,128)(2,1)}, u32[]{:S(2)}, u32[]{:S(2)}) collective-permute-start(bf16[192,1536]{1,0:T(8,128)(2,1)} %fusion.23), channel_id=1, source_target_pairs={{0,8},{4,12},{8,0},{12,4},{1,9},{5,13},{9,1},{13,5},{2,10},{6,14},... | collective-permute-start | bytes 1769480 | tf_op jit(solution)/shard_map/ppermute | solution.py:212
  219.3 2.4 bitcast_add_fusion.1
  225.0 2.0 convolution_add_fusion.1
  230.5 1.9 slice.403
  238.2 1.8 bitcast_add_fusion.3
  242.0 2.0 collective-permute-start.45
  245.9 2.7 collective-permute-start.30
  248.8 3.4 %collective-permute-done.30 = f32[7680]{0:T(1024)S(1)} collective-permute-done((f32[7680]{0:T(1024)S(1)}, f32[7680]{0:T(1024)S(1)}, u32[]{:S(2)}, u32[]{:S(2)}) %collective-permute-start.30) | collective-permute-done | bytes 30752 | tf_op jit(solution)/shard_map/ppermute | solution.py:212
  254.3 1.7 collective-permute-start.27
  256.1 2.0 collective-permute-start.32
  259.4 7.3 %collective-permute-done.32 = f32[7680]{0:T(1024)S(1)} collective-permute-done((f32[7680]{0:T(1024)S(1)}, f32[7680]{0:T(1024)S(1)}, u32[]{:S(2)}, u32[]{:S(2)}) %collective-permute-start.32) | collective-permute-done | bytes 30752 | tf_op jit(solution)/shard_map/ppermute | solution.py:224
  266.7 2.2 collective-permute-start.33
  268.9 3.9 %copy.43 = bf16[4,256,767]{1,0,2:T(4,128)(2,1)} copy(bf16[4,256,767]{2,1,0:T(8,128)(2,1)} %bitcast.172) | data formatting | bytes 3141632
  272.8 1.7 collective-permute-start.35
  284.3 2.7 collective-permute-done.37
  287.4 2.1 collective-permute-start.28
  289.5 7.7 %collective-permute-done.38 = bf16[192,768]{1,0:T(8,128)(2,1)S(1)} collective-permute-done((bf16[192,768]{1,0:T(8,128)(2,1)S(1)}, bf16[192,768]{1,0:T(8,128)(2,1)S(1)}, u32[]{:S(2)}, u32[]{:S(2)}) %collective-permute-start.38) | collective-permute-done | bytes 294944 | tf_op jit(solution)/shard_map/ppermute | solution.py:224
  298.9 2.5 collective-permute-start.40
  301.4 19.1 %collective-permute-done.28 = bf16[2,256,768]{2,1,0:T(8,128)(2,1)S(1)} collective-permute-done((bf16[2,256,768]{2,1,0:T(8,128)(2,1)S(1)}, bf16[2,256,768]{2,1,0:T(8,128)(2,1)S(1)}, u32[]{:S(2)}, u32[]{:S(2)}) %collective-permute-start.28) | collective-permute-done | bytes 786464 | tf_op jit(solution)/shard_map/ppermute | solution.py:224
  321.0 2.2 copy.44
  (353 shorter events, 90.6 us)
Async XLA Ops:
  2.1 13.6 %collective-permute-start.6 = (f32[1152]{0:T(1024)S(1)}, f32[1152]{0:T(1024)S(1)}, u32[]{:S(2)}, u32[]{:S(2)}) collective-permute-start(f32[1152]{0:T(1024)S(1)} %constant_dynamic-update-slice_fusion.9), channel_id=1, source_target_pairs={{0,2},{1,3},{2,0},{3,1},{4,6},{5,7},{6,4},{7,5},{8,10},{9,11},{10,... | collective-permute-start | bytes 13832 | tf_op jit(solution)/shard_map/ppermute | solution.py:224
  8.1 12.3 %collective-permute-start = (bf16[96,768]{1,0:T(8,128)(2,1)S(1)}, bf16[96,768]{1,0:T(8,128)(2,1)S(1)}, u32[]{:S(2)}, u32[]{:S(2)}) collective-permute-start(bf16[96,768]{1,0:T(8,128)(2,1)S(1)} %pad_maximum_fusion.33), channel_id=1, source_target_pairs={{0,2},{1,3},{2,0},{3,1},{4,6},{5,7},{6,4},{7,5},{8,10},{9,11},{10,... | collective-permute-start | bytes 442376 | tf_op jit(solution)/shard_map/ppermute | solution.py:224
  15.8 4.3 %collective-permute-start.7 = (f32[1152]{0:T(1024)S(1)}, f32[1152]{0:T(1024)S(1)}, u32[]{:S(2)}, u32[]{:S(2)}) collective-permute-start(f32[1152]{0:T(1024)S(1)} %broadcast_select_fusion.12), channel_id=1, source_target_pairs={{0,1},{1,0},{2,3},{3,2},{4,5},{5,4},{6,7},{7,6},{8,9},{9,8},{10,11... | collective-permute-start | bytes 13832 | tf_op jit(solution)/shard_map/ppermute | solution.py:224
  20.7 1.4 collective-permute-start.2
  22.3 9.1 %collective-permute-start.3 = (bf16[192,768]{1,0:T(8,128)(2,1)S(1)}, bf16[192,768]{1,0:T(8,128)(2,1)S(1)}, u32[]{:S(2)}, u32[]{:S(2)}) collective-permute-start(bf16[192,768]{1,0:T(8,128)(2,1)S(1)} %bitcast.194), channel_id=1, source_target_pairs={{0,1},{1,0},{2,3},{3,2},{4,5},{5,4},{6,7},{7,6},{8,9},{9,8},{10,11... | collective-permute-start | bytes 884744 | tf_op jit(solution)/shard_map/ppermute | solution.py:224
  23.8 26.9 %collective-permute-start.1 = (bf16[256,1536]{1,0:T(8,128)(2,1)S(1)}, bf16[256,1536]{1,0:T(8,128)(2,1)S(1)}, u32[]{:S(2)}, u32[]{:S(2)}) collective-permute-start(bf16[256,1536]{1,0:T(8,128)(2,1)S(1)} %pad_maximum_fusion.11), channel_id=1, source_target_pairs={{0,4},{4,0},{8,12},{12,8},{1,5},{5,1},{9,13},{13,9},{2,6},{6,2},{1... | collective-permute-start | bytes 2359304 | tf_op jit(solution)/shard_map/ppermute | solution.py:209
  31.5 15.4 %collective-permute-start.13 = (bf16[96,1536]{1,0:T(8,128)(2,1)S(1)}, bf16[96,1536]{1,0:T(8,128)(2,1)S(1)}, u32[]{:S(2)}, u32[]{:S(2)}) collective-permute-start(bf16[96,1536]{1,0:T(8,128)(2,1)S(1)} %pad_maximum_fusion.30), channel_id=1, source_target_pairs={{0,2},{1,3},{2,0},{3,1},{4,6},{5,7},{6,4},{7,5},{8,10},{9,11},{10,... | collective-permute-start | bytes 884744 | tf_op jit(solution)/shard_map/ppermute | solution.py:224
  34.3 12.7 %collective-permute-start.4 = (bf16[192,768]{1,0:T(8,128)(2,1)S(1)}, bf16[192,768]{1,0:T(8,128)(2,1)S(1)}, u32[]{:S(2)}, u32[]{:S(2)}) collective-permute-start(bf16[192,768]{1,0:T(8,128)(2,1)S(1)} %pad_maximum_fusion.28), channel_id=1, source_target_pairs={{0,16},{16,0},{1,17},{17,1},{2,18},{18,2},{3,19},{19,3},{4,20},{20... | collective-permute-start | bytes 884744 | tf_op jit(solution)/shard_map/ppermute | solution.py:221
  36.0 12.8 %collective-permute-start.8 = (bf16[192,768]{1,0:T(8,128)(2,1)S(1)}, bf16[192,768]{1,0:T(8,128)(2,1)S(1)}, u32[]{:S(2)}, u32[]{:S(2)}) collective-permute-start(bf16[192,768]{1,0:T(8,128)(2,1)S(1)} %pad_maximum_fusion.29), channel_id=1, source_target_pairs={{0,8},{4,12},{8,0},{12,4},{1,9},{5,13},{9,1},{13,5},{2,10},{6,14},... | collective-permute-start | bytes 884744 | tf_op jit(solution)/shard_map/ppermute | solution.py:212
  46.9 3.9 %collective-permute-start.14 = (bf16[96,1536]{1,0:T(8,128)(2,1)S(1)}, bf16[96,1536]{1,0:T(8,128)(2,1)S(1)}, u32[]{:S(2)}, u32[]{:S(2)}) collective-permute-start(bf16[96,1536]{1,0:T(8,128)(2,1)S(1)} %broadcast_select_fusion), channel_id=1, source_target_pairs={{0,4},{4,0},{8,12},{12,8},{1,5},{5,1},{9,13},{13,9},{2,6},{6,2},{1... | collective-permute-start | bytes 884744 | tf_op jit(solution)/shard_map/ppermute | solution.py:209
  47.3 22.0 %collective-permute-start.5 = (bf16[2,192,768]{2,1,0:T(8,128)(2,1)S(1)}, bf16[2,192,768]{2,1,0:T(8,128)(2,1)S(1)}, u32[]{:S(2)}, u32[]{:S(2)}) collective-permute-start(bf16[2,192,768]{2,1,0:T(8,128)(2,1)S(1)} %pad_maximum_fusion.17), channel_id=1, source_target_pairs={{0,8},{4,12},{8,0},{12,4},{1,9},{5,13},{9,1},{13,5},{2,10},{6,14},... | collective-permute-start | bytes 1769480 | tf_op jit(solution)/shard_map/ppermute | solution.py:212
  49.1 15.5 %collective-permute-start.9 = (bf16[2,192,768]{2,1,0:T(8,128)(2,1)S(1)}, bf16[2,192,768]{2,1,0:T(8,128)(2,1)S(1)}, u32[]{:S(2)}, u32[]{:S(2)}) collective-permute-start(bf16[2,192,768]{2,1,0:T(8,128)(2,1)S(1)} %pad_maximum_fusion.18), channel_id=1, source_target_pairs={{0,16},{16,0},{1,17},{17,1},{2,18},{18,2},{3,19},{19,3},{4,20},{20... | collective-permute-start | bytes 1769480 | tf_op jit(solution)/shard_map/ppermute | solution.py:221
  51.0 18.7 %collective-permute-start.15 = (bf16[192,1536]{1,0:T(8,128)(2,1)S(1)}, bf16[192,1536]{1,0:T(8,128)(2,1)S(1)}, u32[]{:S(2)}, u32[]{:S(2)}) collective-permute-start(bf16[192,1536]{1,0:T(8,128)(2,1)S(1)} %bitcast.192), channel_id=1, source_target_pairs={{0,1},{1,0},{2,3},{3,2},{4,5},{5,4},{6,7},{7,6},{8,9},{9,8},{10,11... | collective-permute-start | bytes 1769480 | tf_op jit(solution)/shard_map/ppermute | solution.py:224
  65.9 20.3 %collective-permute-start.10 = (bf16[512,768]{1,0:T(8,128)(2,1)S(1)}, bf16[512,768]{1,0:T(8,128)(2,1)}, u32[]{:S(2)}, u32[]{:S(2)}) collective-permute-start(bf16[512,768]{1,0:T(8,128)(2,1)S(1)} %add_convert_fusion.k_ref.v_ref), channel_id=1, source_target_pairs={{0,8},{4,12},{1,9},{5,13},{2,10},{6,14},{3,11},{7,15},{16,24},{20,... | collective-permute-start | bytes 2359304 | tf_op jit(solution)/shard_map/ppermute | solution.py:215
  70.9 27.5 %collective-permute-start.16 = (bf16[192,1536]{1,0:T(8,128)(2,1)}, bf16[192,1536]{1,0:T(8,128)(2,1)}, u32[]{:S(2)}, u32[]{:S(2)}) collective-permute-start(bf16[192,1536]{1,0:T(8,128)(2,1)} %get-tuple-element.40), channel_id=1, source_target_pairs={{0,8},{4,12},{8,0},{12,4},{1,9},{5,13},{9,1},{13,5},{2,10},{6,14},... | collective-permute-start | bytes 1769480 | tf_op jit(solution)/shard_map/ppermute | solution.py:212
  72.2 29.2 %collective-permute-start.18 = (bf16[192,1536]{1,0:T(8,128)(2,1)S(1)}, bf16[192,1536]{1,0:T(8,128)(2,1)}, u32[]{:S(2)}, u32[]{:S(2)}) collective-permute-start(bf16[192,1536]{1,0:T(8,128)(2,1)S(1)} %get-tuple-element.41), channel_id=1, source_target_pairs={{0,16},{16,0},{1,17},{17,1},{2,18},{18,2},{3,19},{19,3},{4,20},{20... | collective-permute-start | bytes 1769480 | tf_op jit(solution)/shard_map/ppermute | solution.py:221
  98.3 7.1 %collective-permute-start.11 = (bf16[256,768]{1,0:T(8,128)(2,1)S(1)}, bf16[256,768]{1,0:T(8,128)(2,1)S(1)}, u32[]{:S(2)}, u32[]{:S(2)}) collective-permute-start(bf16[256,768]{1,0:T(8,128)(2,1)S(1)} %slice.406), channel_id=1, source_target_pairs={{0,4},{4,0},{8,12},{12,8},{1,5},{5,1},{9,13},{13,9},{2,6},{6,2},{1... | collective-permute-start | bytes 1179656 | tf_op jit(solution)/shard_map/ppermute | solution.py:209
  99.9 28.4 %collective-permute-start.17 = (bf16[2,192,1536]{2,1,0:T(8,128)(2,1)S(1)}, bf16[2,192,1536]{2,1,0:T(8,128)(2,1)S(1)}, u32[]{:S(2)}, u32[]{:S(2)}) collective-permute-start(bf16[2,192,1536]{2,1,0:T(8,128)(2,1)S(1)} %pad_maximum_fusion.8), channel_id=1, source_target_pairs={{0,16},{16,0},{1,17},{17,1},{2,18},{18,2},{3,19},{19,3},{4,20},{20... | collective-permute-start | bytes 3538952 | tf_op jit(solution)/shard_map/ppermute | solution.py:221
  102.7 29.0 %collective-permute-start.19 = (bf16[2,192,1536]{2,1,0:T(8,128)(2,1)S(1)}, bf16[2,192,1536]{2,1,0:T(8,128)(2,1)S(1)}, u32[]{:S(2)}, u32[]{:S(2)}) collective-permute-start(bf16[2,192,1536]{2,1,0:T(8,128)(2,1)S(1)} %pad_maximum_fusion.9), channel_id=1, source_target_pairs={{0,8},{4,12},{8,0},{12,4},{1,9},{5,13},{9,1},{13,5},{2,10},{6,14},... | collective-permute-start | bytes 3538952 | tf_op jit(solution)/shard_map/ppermute | solution.py:212
  106.4 25.9 %collective-permute-start.12 = (bf16[256,768]{1,0:T(8,128)(2,1)S(1)}, bf16[256,768]{1,0:T(8,128)(2,1)S(1)}, u32[]{:S(2)}, u32[]{:S(2)}) collective-permute-start(bf16[256,768]{1,0:T(8,128)(2,1)S(1)} %multiply_convert_fusion.1), channel_id=1, source_target_pairs={{0,4},{4,0},{8,12},{12,8},{1,5},{5,1},{9,13},{13,9},{2,6},{6,2},{1... | collective-permute-start | bytes 1179656 | tf_op jit(solution)/shard_map/ppermute | solution.py:209
  146.0 13.5 %collective-permute-start.20 = (bf16[256,768]{1,0:T(8,128)(2,1)S(1)}, bf16[256,768]{1,0:T(8,128)(2,1)S(1)}, u32[]{:S(2)}, u32[]{:S(2)}) collective-permute-start(bf16[256,768]{1,0:T(8,128)(2,1)S(1)} %slice.405), channel_id=1, source_target_pairs={{0,4},{4,0},{8,12},{12,8},{1,5},{5,1},{9,13},{13,9},{2,6},{6,2},{1... | collective-permute-start | bytes 1179656 | tf_op jit(solution)/shard_map/ppermute | solution.py:209
  146.1 13.6 %collective-permute-start.22 = (bf16[256,768]{1,0:T(8,128)(2,1)}, bf16[256,768]{1,0:T(8,128)(2,1)S(1)}, u32[]{:S(2)}, u32[]{:S(2)}) collective-permute-start(bf16[256,768]{1,0:T(8,128)(2,1)} %slice.404), channel_id=1, source_target_pairs={{0,4},{4,0},{8,12},{12,8},{1,5},{5,1},{9,13},{13,9},{2,6},{6,2},{1... | collective-permute-start | bytes 1179656 | tf_op jit(solution)/shard_map/ppermute | solution.py:209
  152.5 60.0 %collective-permute-start.43 = (bf16[2,192,1536]{2,1,0:T(8,128)(2,1)}, bf16[2,192,1536]{2,1,0:T(8,128)(2,1)}, u32[]{:S(2)}, u32[]{:S(2)}) collective-permute-start(bf16[2,192,1536]{2,1,0:T(8,128)(2,1)} %fusion.10), channel_id=1, source_target_pairs={{0,16},{16,0},{1,17},{17,1},{2,18},{18,2},{3,19},{19,3},{4,20},{20... | collective-permute-start | bytes 3538952 | tf_op jit(solution)/shard_map/ppermute | solution.py:221
  157.8 61.6 %collective-permute-start.41 = (bf16[2,192,1536]{2,1,0:T(8,128)(2,1)}, bf16[2,192,1536]{2,1,0:T(8,128)(2,1)}, u32[]{:S(2)}, u32[]{:S(2)}) collective-permute-start(bf16[2,192,1536]{2,1,0:T(8,128)(2,1)} %fusion.9), channel_id=1, source_target_pairs={{0,8},{4,12},{8,0},{12,4},{1,9},{5,13},{9,1},{13,5},{2,10},{6,14},... | collective-permute-start | bytes 3538952 | tf_op jit(solution)/shard_map/ppermute | solution.py:212
  161.1 20.2 %collective-permute-start.21 = (bf16[256,768]{1,0:T(8,128)(2,1)S(1)}, bf16[256,768]{1,0:T(8,128)(2,1)S(1)}, u32[]{:S(2)}, u32[]{:S(2)}) collective-permute-start(bf16[256,768]{1,0:T(8,128)(2,1)S(1)} %get-tuple-element.126), channel_id=1, source_target_pairs={{0,2},{1,3},{2,0},{3,1},{4,6},{5,7},{6,4},{7,5},{8,10},{9,11},{10,... | collective-permute-start | bytes 1179656 | tf_op jit(solution)/shard_map/ppermute | solution.py:224
  162.0 20.4 %collective-permute-start.23 = (bf16[256,768]{1,0:T(8,128)(2,1)S(1)}, bf16[256,768]{1,0:T(8,128)(2,1)S(1)}, u32[]{:S(2)}, u32[]{:S(2)}) collective-permute-start(bf16[256,768]{1,0:T(8,128)(2,1)S(1)} %get-tuple-element.101), channel_id=1, source_target_pairs={{0,4},{4,0},{8,12},{12,8},{1,5},{5,1},{9,13},{13,9},{2,6},{6,2},{1... | collective-permute-start | bytes 1179656 | tf_op jit(solution)/shard_map/ppermute | solution.py:209
  200.0 23.4 %collective-permute-start.25 = (bf16[512,768]{1,0:T(8,128)(2,1)}, bf16[512,768]{1,0:T(8,128)(2,1)}, u32[]{:S(2)}, u32[]{:S(2)}) collective-permute-start(bf16[512,768]{1,0:T(8,128)(2,1)} %pad_maximum_fusion.15), channel_id=1, source_target_pairs={{8,0},{12,4},{9,1},{13,5},{10,2},{14,6},{11,3},{15,7},{24,16},{28,... | collective-permute-start | bytes 2359304 | tf_op jit(solution)/shard_map/ppermute | solution.py:218
  201.3 25.6 %collective-permute-start.24 = (bf16[2,256,768]{2,1,0:T(8,128)(2,1)}, bf16[2,256,768]{2,1,0:T(8,128)(2,1)}, u32[]{:S(2)}, u32[]{:S(2)}) collective-permute-start(bf16[2,256,768]{2,1,0:T(8,128)(2,1)} %pad_maximum_fusion.13), channel_id=1, source_target_pairs={{0,1},{1,0},{2,3},{3,2},{4,5},{5,4},{6,7},{7,6},{8,9},{9,8},{10,11... | collective-permute-start | bytes 2359304 | tf_op jit(solution)/shard_map/ppermute | solution.py:224
  210.7 45.4 %collective-permute-start.34 = (bf16[2,192,768]{2,1,0:T(8,128)(2,1)}, bf16[2,192,768]{2,1,0:T(8,128)(2,1)}, u32[]{:S(2)}, u32[]{:S(2)}) collective-permute-start(bf16[2,192,768]{2,1,0:T(8,128)(2,1)} %fusion.21), channel_id=1, source_target_pairs={{0,16},{16,0},{1,17},{17,1},{2,18},{18,2},{3,19},{19,3},{4,20},{20... | collective-permute-start | bytes 1769480 | tf_op jit(solution)/shard_map/ppermute | solution.py:221
  215.8 20.6 %collective-permute-start.44 = (bf16[192,1536]{1,0:T(8,128)(2,1)}, bf16[192,1536]{1,0:T(8,128)(2,1)}, u32[]{:S(2)}, u32[]{:S(2)}) collective-permute-start(bf16[192,1536]{1,0:T(8,128)(2,1)} %fusion.23), channel_id=1, source_target_pairs={{0,8},{4,12},{8,0},{12,4},{1,9},{5,13},{9,1},{13,5},{2,10},{6,14},... | collective-permute-start | bytes 1769480 | tf_op jit(solution)/shard_map/ppermute | solution.py:212
  222.7 15.5 %collective-permute-start.42 = (bf16[192,1536]{1,0:T(8,128)(2,1)}, bf16[192,1536]{1,0:T(8,128)(2,1)}, u32[]{:S(2)}, u32[]{:S(2)}) collective-permute-start(bf16[192,1536]{1,0:T(8,128)(2,1)} %fusion.22), channel_id=1, source_target_pairs={{0,16},{16,0},{1,17},{17,1},{2,18},{18,2},{3,19},{19,3},{4,20},{20... | collective-permute-start | bytes 1769480 | tf_op jit(solution)/shard_map/ppermute | solution.py:221
  232.5 11.6 %collective-permute-start.26 = (bf16[256,768]{1,0:T(8,128)(2,1)}, bf16[256,768]{1,0:T(8,128)(2,1)S(1)}, u32[]{:S(2)}, u32[]{:S(2)}) collective-permute-start(bf16[256,768]{1,0:T(8,128)(2,1)} %slice.403), channel_id=1, source_target_pairs={{0,4},{4,0},{8,12},{12,8},{1,5},{5,1},{9,13},{13,9},{2,6},{6,2},{1... | collective-permute-start | bytes 1179656 | tf_op jit(solution)/shard_map/ppermute | solution.py:209
  235.6 42.3 %collective-permute-start.36 = (bf16[2,192,768]{2,1,0:T(8,128)(2,1)}, bf16[2,192,768]{2,1,0:T(8,128)(2,1)}, u32[]{:S(2)}, u32[]{:S(2)}) collective-permute-start(bf16[2,192,768]{2,1,0:T(8,128)(2,1)} %fusion.24), channel_id=1, source_target_pairs={{0,8},{4,12},{8,0},{12,4},{1,9},{5,13},{9,1},{13,5},{2,10},{6,14},... | collective-permute-start | bytes 1769480 | tf_op jit(solution)/shard_map/ppermute | solution.py:212
  242.0 39.7 %collective-permute-start.45 = (bf16[192,1536]{1,0:T(8,128)(2,1)}, bf16[192,1536]{1,0:T(8,128)(2,1)}, u32[]{:S(2)}, u32[]{:S(2)}) collective-permute-start(bf16[192,1536]{1,0:T(8,128)(2,1)} %pad_maximum_fusion.22), channel_id=1, source_target_pairs={{0,1},{1,0},{2,3},{3,2},{4,5},{5,4},{6,7},{7,6},{8,9},{9,8},{10,11... | collective-permute-start | bytes 1769480 | tf_op jit(solution)/shard_map/ppermute | solution.py:224
  244.6 1.3 collective-permute-start.29
  245.9 6.3 %collective-permute-start.30 = (f32[7680]{0:T(1024)S(1)}, f32[7680]{0:T(1024)S(1)}, u32[]{:S(2)}, u32[]{:S(2)}) collective-permute-start(f32[7680]{0:T(1024)S(1)} %add.287), channel_id=1, source_target_pairs={{0,8},{4,12},{8,0},{12,4},{1,9},{5,13},{9,1},{13,5},{2,10},{6,14},... | collective-permute-start | bytes 92168 | tf_op jit(solution)/shard_map/ppermute | solution.py:212
  252.2 3.9 %collective-permute-start.31 = (f32[7680]{0:T(1024)S(1)}, f32[7680]{0:T(1024)S(1)}, u32[]{:S(2)}, u32[]{:S(2)}) collective-permute-start(f32[7680]{0:T(1024)S(1)} %add.288), channel_id=1, source_target_pairs={{0,16},{16,0},{1,17},{17,1},{2,18},{18,2},{3,19},{19,3},{4,20},{20... | collective-permute-start | bytes 92168 | tf_op jit(solution)/shard_map/ppermute | solution.py:221
  254.3 28.8 %collective-permute-start.27 = (bf16[256,768]{1,0:T(8,128)(2,1)}, bf16[256,768]{1,0:T(8,128)(2,1)}, u32[]{:S(2)}, u32[]{:S(2)}) collective-permute-start(bf16[256,768]{1,0:T(8,128)(2,1)} %subtract_convert_fusion), channel_id=1, source_target_pairs={{0,2},{1,3},{2,0},{3,1},{4,6},{5,7},{6,4},{7,5},{8,10},{9,11},{10,... | collective-permute-start | bytes 1179656 | tf_op jit(solution)/shard_map/ppermute | solution.py:224
  256.1 10.5 %collective-permute-start.32 = (f32[7680]{0:T(1024)S(1)}, f32[7680]{0:T(1024)S(1)}, u32[]{:S(2)}, u32[]{:S(2)}) collective-permute-start(f32[7680]{0:T(1024)S(1)} %add.289), channel_id=1, source_target_pairs={{0,1},{1,0},{2,3},{3,2},{4,5},{5,4},{6,7},{7,6},{8,9},{9,8},{10,11... | collective-permute-start | bytes 92168 | tf_op jit(solution)/shard_map/ppermute | solution.py:224
  266.7 9.1 %collective-permute-start.33 = (f32[7680]{0:T(1024)S(1)}, f32[7680]{0:T(1024)S(1)}, u32[]{:S(2)}, u32[]{:S(2)}) collective-permute-start(f32[7680]{0:T(1024)S(1)} %add.290), channel_id=1, source_target_pairs={{0,2},{1,3},{2,0},{3,1},{4,6},{5,7},{6,4},{7,5},{8,10},{9,11},{10,... | collective-permute-start | bytes 92168 | tf_op jit(solution)/shard_map/ppermute | solution.py:224
  272.8 7.7 %collective-permute-start.35 = (bf16[192,768]{1,0:T(8,128)(2,1)S(1)}, bf16[192,768]{1,0:T(8,128)(2,1)}, u32[]{:S(2)}, u32[]{:S(2)}) collective-permute-start(bf16[192,768]{1,0:T(8,128)(2,1)S(1)} %fusion.43), channel_id=1, source_target_pairs={{0,8},{4,12},{8,0},{12,4},{1,9},{5,13},{9,1},{13,5},{2,10},{6,14},... | collective-permute-start | bytes 884744 | tf_op jit(solution)/shard_map/ppermute | solution.py:212
  279.2 7.8 %collective-permute-start.37 = (bf16[192,768]{1,0:T(8,128)(2,1)S(1)}, bf16[192,768]{1,0:T(8,128)(2,1)S(1)}, u32[]{:S(2)}, u32[]{:S(2)}) collective-permute-start(bf16[192,768]{1,0:T(8,128)(2,1)S(1)} %fusion.44), channel_id=1, source_target_pairs={{0,16},{16,0},{1,17},{17,1},{2,18},{18,2},{3,19},{19,3},{4,20},{20... | collective-permute-start | bytes 884744 | tf_op jit(solution)/shard_map/ppermute | solution.py:221
  283.0 14.5 %collective-permute-start.46 = (bf16[96,1536]{1,0:T(8,128)(2,1)S(1)}, bf16[96,1536]{1,0:T(8,128)(2,1)S(1)}, u32[]{:S(2)}, u32[]{:S(2)}) collective-permute-start(bf16[96,1536]{1,0:T(8,128)(2,1)S(1)} %fusion.45), channel_id=1, source_target_pairs={{0,4},{4,0},{8,12},{12,8},{1,5},{5,1},{9,13},{13,9},{2,6},{6,2},{1... | collective-permute-start | bytes 884744 | tf_op jit(solution)/shard_map/ppermute | solution.py:209
  287.3 9.9 %collective-permute-start.38 = (bf16[192,768]{1,0:T(8,128)(2,1)S(1)}, bf16[192,768]{1,0:T(8,128)(2,1)S(1)}, u32[]{:S(2)}, u32[]{:S(2)}) collective-permute-start(bf16[192,768]{1,0:T(8,128)(2,1)S(1)} %pad_maximum_fusion.31), channel_id=1, source_target_pairs={{0,1},{1,0},{2,3},{3,2},{4,5},{5,4},{6,7},{7,6},{8,9},{9,8},{10,11... | collective-permute-start | bytes 884744 | tf_op jit(solution)/shard_map/ppermute | solution.py:224
  287.4 33.1 %collective-permute-start.28 = (bf16[2,256,768]{2,1,0:T(8,128)(2,1)S(1)}, bf16[2,256,768]{2,1,0:T(8,128)(2,1)S(1)}, u32[]{:S(2)}, u32[]{:S(2)}) collective-permute-start(bf16[2,256,768]{2,1,0:T(8,128)(2,1)S(1)} %pad_maximum_fusion.16), channel_id=1, source_target_pairs={{0,1},{1,0},{2,3},{3,2},{4,5},{5,4},{6,7},{7,6},{8,9},{9,8},{10,11... | collective-permute-start | bytes 2359304 | tf_op jit(solution)/shard_map/ppermute | solution.py:224
  297.4 1.4 collective-permute-start.39
  298.3 25.7 %collective-permute-start.47 = (bf16[96,1536]{1,0:T(8,128)(2,1)}, bf16[96,1536]{1,0:T(8,128)(2,1)}, u32[]{:S(2)}, u32[]{:S(2)}) collective-permute-start(bf16[96,1536]{1,0:T(8,128)(2,1)} %fusion.20), channel_id=1, source_target_pairs={{0,2},{1,3},{2,0},{3,1},{4,6},{5,7},{6,4},{7,5},{8,10},{9,11},{10,... | collective-permute-start | bytes 884744 | tf_op jit(solution)/shard_map/ppermute | solution.py:224
  298.9 22.0 %collective-permute-start.40 = (bf16[96,768]{1,0:T(8,128)(2,1)S(1)}, bf16[96,768]{1,0:T(8,128)(2,1)S(1)}, u32[]{:S(2)}, u32[]{:S(2)}) collective-permute-start(bf16[96,768]{1,0:T(8,128)(2,1)S(1)} %fusion.42), channel_id=1, source_target_pairs={{0,2},{1,3},{2,0},{3,1},{4,6},{5,7},{6,4},{7,5},{8,10},{9,11},{10,... | collective-permute-start | bytes 442376 | tf_op jit(solution)/shard_map/ppermute | solution.py:224
  (61 other events, 435.6 us)
